TPU v7x, 512 devices: a whole 4x8x8 slice. The times are simulated.
512 devices in a mesh: pole: 16 (over x, z_lo, core), slab: 32 (over y, z_hi).
Axes of the slice: x: 4, y: 8, z: 8 (z_hi: 4, z_lo: 2; z = z_hi * 2 + z_lo), core: 2. Of those that a mesh axis runs over, the one named last changes fastest.
Arguments:
- vectors: float32 [2, 16, 128, 16, 128], P(None, None, 'slab'), may hold values from -6 to 6
- potential: float32 [128, 16, 128], P('slab'), may hold values from 0 to 2
Outputs:
- filtered: float32 [2, 16, 128, 16, 128], P(None, None, 'slab', 'pole')
- gram_correlation: float32 [2, 16, 16], replicated
- gram_energy: float32 [2, 16, 16], replicated
All inputs are finite; a program needn't handle non-finite values.
Results may differ from a plain program's by a relative error of at most 0.005.
Values sent between devices are 32-bit elements; how exact they have to be, the bound alone decides.
No kernel may reach another device: no remote copies, remote signals or barrier semaphores. Data moves between devices by JAX's collectives and lax.ppermute only.
A program may use at most 64 MiB of HBM per device.

v0:
```python
import math

import jax
import jax.numpy as jnp
from jax import lax
from jax.sharding import PartitionSpec as P

ITERS = 3


contour_center = 2.0
contour_radius = 1.5


def extended(block, sides, width):
    for axis, dim in sides:
        count = lax.axis_size(axis)
        forward = [(i, i + 1) for i in range(count - 1)]
        forward.append((count - 1, 0))
        backward = [(target, source) for source, target in forward]
        low = lax.ppermute(
            lax.slice_in_dim(block, block.shape[dim] - width, None, axis=dim), axis, forward
        )
        high = lax.ppermute(lax.slice_in_dim(block, 0, width, axis=dim), axis, backward)
        block = jnp.concatenate([low, block, high], axis=dim)
    return block


def apply_shifted(block, potential, shift_re, shift_im):
    padded = extended(block, (("slab", 2),), 1)
    beside = padded[:, :, 2:] + padded[:, :, :-2]
    beside = beside + jnp.roll(block, 1, 3) + jnp.roll(block, -1, 3)
    beside = beside + jnp.roll(block, 1, 4) + jnp.roll(block, -1, 4)
    diagonal = shift_re - 3.0 - potential
    real_part = diagonal * block[0] - shift_im * block[1] + 0.5 * beside[0]
    imag_part = diagonal * block[1] + shift_im * block[0] + 0.5 * beside[1]
    return jnp.stack([real_part, imag_part])


def bilinear(left, right):
    real_part = jnp.sum(left[0] * right[0] - left[1] * right[1], axis=(1, 2, 3))
    imag_part = jnp.sum(left[0] * right[1] + left[1] * right[0], axis=(1, 2, 3))
    return jnp.stack([real_part, imag_part])


def complex_divide(numer, denom):
    magnitude = denom[0] * denom[0] + denom[1] * denom[1]
    return jnp.stack(
        [
            (numer[0] * denom[0] + numer[1] * denom[1]) / magnitude,
            (numer[1] * denom[0] - numer[0] * denom[1]) / magnitude,
        ]
    )


def column_scale(coef, block):
    first = coef[0][:, None, None, None]
    second = coef[1][:, None, None, None]
    return jnp.stack([first * block[0] - second * block[1], first * block[1] + second * block[0]])


def scalar_scale(first, second, block):
    return jnp.stack([first * block[0] - second * block[1], first * block[1] + second * block[0]])


def inner(left, right):
    return lax.dot_general(
        left,
        right,
        (((1,), (1,)), ((), ())),
        precision=lax.Precision.HIGHEST,
        preferred_element_type=jnp.float32,
    )


def gram_pair(filtered, image, cells):
    count = filtered.shape[1]
    sre = filtered[0].reshape(count, -1)
    sim = filtered[1].reshape(count, -1)
    hre = image[0].reshape(count, -1)
    him = image[1].reshape(count, -1)
    correlation = (
        jnp.stack([inner(sre, sre) + inner(sim, sim), inner(sre, sim) - inner(sim, sre)]) / cells
    )
    energy = (
        jnp.stack([inner(sre, hre) + inner(sim, him), inner(sre, him) - inner(sim, hre)]) / cells
    )
    return (correlation, energy)


def residual_form(residual):
    return lax.psum(bilinear(residual, residual), "slab")


def on_device(vectors, potential):
    pole_count = lax.axis_size("pole")
    angle = 2.0 * math.pi / pole_count * (lax.axis_index("pole").astype(jnp.float32) + 0.5)
    cosine = jnp.cos(angle)
    sine = jnp.sin(angle)
    shift_re = contour_center + contour_radius * cosine
    shift_im = contour_radius * sine
    weight_re = contour_radius * cosine / pole_count
    weight_im = contour_radius * sine / pole_count
    solution = jnp.zeros_like(vectors)
    residual = vectors
    direction = vectors
    rho = residual_form(residual)
    for iteration in range(ITERS):
        mapped = apply_shifted(direction, potential, shift_re, shift_im)
        curve = lax.psum(bilinear(direction, mapped), "slab")
        alpha = complex_divide(rho, curve)
        solution = solution + column_scale(alpha, direction)
        residual = residual - column_scale(alpha, mapped)
        if iteration + 1 < ITERS:
            rho_new = residual_form(residual)
            direction = residual + column_scale(complex_divide(rho_new, rho), direction)
            rho = rho_new
    weighted = scalar_scale(weight_re, weight_im, solution)
    hsol = scalar_scale(shift_re, shift_im, solution) - vectors + residual
    weighted_image = scalar_scale(weight_re, weight_im, hsol)
    cells = vectors.shape[2] * lax.axis_size("slab") * vectors.shape[3] * vectors.shape[4]
    filtered, image = lax.psum((weighted, weighted_image), "pole")
    correlation, energy = gram_pair(filtered, image, cells)
    correlation, energy = lax.psum((correlation, energy), "slab")
    rows = filtered.shape[3] // pole_count
    own = lax.dynamic_slice_in_dim(filtered, lax.axis_index("pole") * rows, rows, 3)
    return (own, correlation, energy)


def solution(mesh):
    in_specs = (P(None, None, "slab", None, None), P("slab", None, None))
    out_specs = (P(None, None, "slab", "pole", None), P(), P())
    return jax.shard_map(
        on_device, mesh=mesh, in_specs=in_specs, out_specs=out_specs, check_vma=False
    )
```

profile of v0, /device:TPU:32, one launch (start us, length us, event | category | flops | bytes accessed | tf_op | source)
XLA Modules:
  0.0 801.4 jit_solution(13384978102229270736)
XLA Ops:
  7.2 1.8 copy.5
  9.1 10.8 %collective-permute-start = (f32[2,16,1,16,128]{4,1,3,2,0:T(8,128)S(1)}, f32[2,16,1,16,128]{4,1,3,2,0:T(8,128)S(1)}, u32[]{:S(2)}, u32[]{:S(2)}) collective-permute-start(f32[2,16,1,16,128]{4,1,3,2,0:T(8,128)S(1)} %get-tuple-element.77), channel_id=1, source_target_pairs={{1,0},{2,1},{3,2},{4,3},{5,4},{6,5},{7,6},{8,7},{9,8},{10,9},{11,1... | collective-permute-start | bytes 786440 | tf_op jit(solution)/shard_map/ppermute | solution.py:24
  19.9 1.9 collective-permute-start.1
  21.9 1.5 fusion.68
  23.3 1.6 fusion.67
  25.0 1.7 fusion.66
  26.8 2.0 collective-permute-done
  28.8 10.6 %collective-permute-done.1 = f32[2,16,1,16,128]{4,1,3,2,0:T(8,128)S(1)} collective-permute-done((f32[2,16,1,16,128]{4,1,3,2,0:T(8,128)S(1)}, f32[2,16,1,16,128]{4,1,3,2,0:T(8,128)S(1)}, u32[]{:S(2)}, u32[]{:S(2)}) %collective-permute-start.1) | collective-permute-done | bytes 262176 | tf_op jit(solution)/shard_map/ppermute | solution.py:21
  39.4 3.4 fusion.22
  43.5 76.9 %all-reduce.1 = (f32[2,16]{1,0:T(2,128)S(1)}, f32[2,16]{1,0:T(2,128)S(1)}) all-reduce(f32[2,16]{1,0:T(2,128)S(1)} %get-tuple-element.90, f32[2,16]{1,0:T(2,128)S(1)} %get-tuple-element.89), channel_id=1, replica_groups=mesh['pole'=16,'slab'=32] {'slab'}, use_global_device_ids=true, to_apply=%region_5.6 | all-reduce | flops 64 | bytes 512 | tf_op jit(solution)/shard_map/psum | solution.py:110
  120.4 1.4 multiply_subtract_fusion.9
  121.9 1.1 copy-done
  123.9 79.8 %psum.72 = f32[2,16]{1,0:T(2,128)S(1)} all-reduce(f32[2,16]{1,0:T(2,128)S(1)} %pad_maximum_fusion.10), channel_id=1, replica_groups=mesh['pole'=16,'slab'=32] {'slab'}, use_global_device_ids=true, to_apply=%region_8.9 | all-reduce | flops 32 | bytes 256 | tf_op jit(solution)/shard_map/psum | solution.py:92
  205.3 3.2 collective-permute-start.2
  208.6 3.5 collective-permute-start.3
  212.3 4.7 collective-permute-done.2
  217.0 6.9 collective-permute-done.3
  225.6 76.8 %psum.73 = f32[2,16]{1,0:T(2,128)S(1)} all-reduce(f32[2,16]{1,0:T(2,128)S(1)} %pad_maximum_fusion.11), channel_id=1, replica_groups=mesh['pole'=16,'slab'=32] {'slab'}, use_global_device_ids=true, to_apply=%region_11.12 | all-reduce | flops 32 | bytes 256 | tf_op jit(solution)/shard_map/psum | solution.py:110
  302.5 2.5 multiply_subtract_fusion.6
  306.8 79.9 %psum.74 = f32[2,16]{1,0:T(2,128)S(1)} all-reduce(f32[2,16]{1,0:T(2,128)S(1)} %pad_maximum_fusion.12), channel_id=1, replica_groups=mesh['pole'=16,'slab'=32] {'slab'}, use_global_device_ids=true, to_apply=%region_14.15 | all-reduce | flops 32 | bytes 256 | tf_op jit(solution)/shard_map/psum | solution.py:92
  389.5 2.9 collective-permute-start.4
  392.4 4.0 collective-permute-start.5
  396.7 4.3 collective-permute-done.4
  401.0 6.6 collective-permute-done.5
  409.3 76.8 %psum.75 = f32[2,16]{1,0:T(2,128)S(1)} all-reduce(f32[2,16]{1,0:T(2,128)S(1)} %pad_maximum_fusion.13), channel_id=1, replica_groups=mesh['pole'=16,'slab'=32] {'slab'}, use_global_device_ids=true, to_apply=%region_17.18 | all-reduce | flops 32 | bytes 256 | tf_op jit(solution)/shard_map/psum | solution.py:110
  486.2 1.6 multiply_subtract_fusion.1
  491.6 1.0 pad_maximum_fusion.7
  492.7 1.1 pad_maximum_fusion.6
  493.8 134.6 %all-reduce.5.cloned.1.call-done = (f32[2,16,4,16,128]{4,1,3,2,0:T(8,128)}, f32[2,16,4,16,128]{4,1,3,2,0:T(8,128)}) async-done(((f32[2,16,4,16,128]{4,1,3,2,0:T(8,128)}, f32[2,16,4,16,128]{4,1,3,2,0:T(8,128)}), (f32[2,16,4,16,128]{4,1,3,2,0:T(8,128)}, f32[2,16,4,16,128]{4,1,3,2,0:T(8,128)})) %all-reduce.5.cloned.1.call-update) | async-done | bytes 2097168 | tf_op jit(solution)/shard_map/psum | solution.py:122
  628.5 2.1 convolution_bitcast_fusion
  630.5 1.8 convolution_bitcast_fusion.2
  638.0 156.6 %all-reduce = (f32[2,16,16]{2,1,0:T(8,128)}, f32[2,16,16]{2,1,0:T(8,128)}) all-reduce(f32[2,16,16]{2,1,0:T(8,128)S(1)} %maximum_multiply_fusion, f32[2,16,16]{2,1,0:T(8,128)S(1)} %maximum_multiply_fusion.1), channel_id=1, replica_groups=mesh['pole'=16,'slab'=32] {'slab'}, use_global_device_ids=true, to_apply=%region_19.20 | all-reduce | flops 1024 | bytes 8192 | tf_op jit(solution)/shard_map/psum | solution.py:124
  (86 shorter events, 21.2 us)
Async XLA Ops:
  7.2 621.3 %all-reduce.5.cloned.1.call-start = ((), (), s32[]{:S(2)}) async-start(), calls=%async_computation | async-start | bytes 4194304 | tf_op jit(solution)/shard_map/psum | solution.py:122
  9.1 19.7 %collective-permute-start = (f32[2,16,1,16,128]{4,1,3,2,0:T(8,128)S(1)}, f32[2,16,1,16,128]{4,1,3,2,0:T(8,128)S(1)}, u32[]{:S(2)}, u32[]{:S(2)}) collective-permute-start(f32[2,16,1,16,128]{4,1,3,2,0:T(8,128)S(1)} %get-tuple-element.77), channel_id=1, source_target_pairs={{1,0},{2,1},{3,2},{4,3},{5,4},{6,5},{7,6},{8,7},{9,8},{10,9},{11,1... | collective-permute-start | bytes 786440 | tf_op jit(solution)/shard_map/ppermute | solution.py:24
  19.9 19.5 %collective-permute-start.1 = (f32[2,16,1,16,128]{4,1,3,2,0:T(8,128)S(1)}, f32[2,16,1,16,128]{4,1,3,2,0:T(8,128)S(1)}, u32[]{:S(2)}, u32[]{:S(2)}) collective-permute-start(f32[2,16,1,16,128]{4,1,3,2,0:T(8,128)S(1)} %get-tuple-element.78), channel_id=1, source_target_pairs={{0,1},{1,2},{2,3},{3,4},{4,5},{5,6},{6,7},{7,8},{8,9},{9,10},{10,1... | collective-permute-start | bytes 786440 | tf_op jit(solution)/shard_map/ppermute | solution.py:21
  25.0 1.8 copy-start.15
  121.8 1.2 copy-start
  205.3 11.6 %collective-permute-start.2 = (f32[2,16,1,16,128]{4,1,3,2,0:T(8,128)S(1)}, f32[2,16,1,16,128]{4,1,3,2,0:T(8,128)S(1)}, u32[]{:S(2)}, u32[]{:S(2)}) collective-permute-start(f32[2,16,1,16,128]{4,1,3,2,0:T(8,128)S(1)} %get-tuple-element.67), channel_id=1, source_target_pairs={{1,0},{2,1},{3,2},{4,3},{5,4},{6,5},{7,6},{8,7},{9,8},{10,9},{11,1... | collective-permute-start | bytes 786440 | tf_op jit(solution)/shard_map/ppermute | solution.py:24
  208.6 15.3 %collective-permute-start.3 = (f32[2,16,1,16,128]{4,1,3,2,0:T(8,128)S(1)}, f32[2,16,1,16,128]{4,1,3,2,0:T(8,128)S(1)}, u32[]{:S(2)}, u32[]{:S(2)}) collective-permute-start(f32[2,16,1,16,128]{4,1,3,2,0:T(8,128)S(1)} %get-tuple-element.68), channel_id=1, source_target_pairs={{0,1},{1,2},{2,3},{3,4},{4,5},{5,6},{6,7},{7,8},{8,9},{9,10},{10,1... | collective-permute-start | bytes 786440 | tf_op jit(solution)/shard_map/ppermute | solution.py:21
  224.6 1.0 copy-start.3
  305.0 0.8 copy-start.7
  305.1 1.4 copy-start.4
  386.7 1.0 copy-start.5
  386.7 1.2 copy-start.8
  389.5 11.5 %collective-permute-start.4 = (f32[2,16,1,16,128]{4,1,3,2,0:T(8,128)S(1)}, f32[2,16,1,16,128]{4,1,3,2,0:T(8,128)S(1)}, u32[]{:S(2)}, u32[]{:S(2)}) collective-permute-start(f32[2,16,1,16,128]{4,1,3,2,0:T(8,128)S(1)} %get-tuple-element.57), channel_id=1, source_target_pairs={{1,0},{2,1},{3,2},{4,3},{5,4},{6,5},{7,6},{8,7},{9,8},{10,9},{11,1... | collective-permute-start | bytes 786440 | tf_op jit(solution)/shard_map/ppermute | solution.py:24
  392.4 15.2 %collective-permute-start.5 = (f32[2,16,1,16,128]{4,1,3,2,0:T(8,128)S(1)}, f32[2,16,1,16,128]{4,1,3,2,0:T(8,128)S(1)}, u32[]{:S(2)}, u32[]{:S(2)}) collective-permute-start(f32[2,16,1,16,128]{4,1,3,2,0:T(8,128)S(1)} %get-tuple-element.58), channel_id=1, source_target_pairs={{0,1},{1,2},{2,3},{3,4},{4,5},{5,6},{6,7},{7,8},{8,9},{9,10},{10,1... | collective-permute-start | bytes 786440 | tf_op jit(solution)/shard_map/ppermute | solution.py:21
  408.3 1.0 copy-start.2
  486.2 1.8 copy-start.14
  487.8 1.0 copy-start.11
  487.8 1.2 copy-start.12
  487.8 1.3 copy-start.13
  489.3 1.0 copy-start.6
  489.4 1.2 copy-start.9
  628.5 2.1 copy-start.1
  632.3 1.6 copy-start.10
Sparse Core Ops, SparseCore 0:
  493.9 134.4 all-reduce.4
where the time goes:
time: 802 us; the launch traced here: 801 us
  blocking collectives  547 us (68%)
  waiting for transfers between devices  170 us (21%)
  starting transfers between devices  26.4 us (3%)
  other arithmetic  20.1 us (3%)
  local copies, waits for them, and re-layouts  15 us (2%)
  between operations  14.6 us (2%)
  matrix products  8.76 us (1%)
    psum x3, blocking collectives, on_device(): curve = lax.psum(bilinear(direction, mapped), 'slab')  231 us
    psum x2, blocking collectives, residual_form(): return lax.psum(bilinear(residual, residual), 'slab')  160 us
    psum x1, blocking collectives, on_device(): correlation, energy = lax.psum((correlation, energy), 'slab')  157 us
    psum x1, waiting for transfers between devices, on_device(): filtered, image = lax.psum((weighted, weighted_image), 'pole')  135 us
    ppermute x3, waiting for transfers between devices, extended(): lax.ppermute(lax.slice_in_dim(block, block.shape[dim] - width, None, axis...  24.2 us
    ppermute x3, starting transfers between devices, extended(): lax.ppermute(lax.slice_in_dim(block, 0, width, axis=dim), axis, backward)  17 us
  transfers between devices with their start and end apart: 7, of which 7 were waited for; matrix products, arithmetic and copies ran while one was open for 1% of the time, Pallas kernels for 0%

commit v1 on v0

v1 whole, which is shorter than its diff:
```python
import functools
import math

import jax
import jax.numpy as jnp
from jax import lax
from jax.experimental import pallas as pl
from jax.experimental.pallas import tpu as pltpu
from jax.sharding import Mesh
from jax.sharding import PartitionSpec as P

contour_center = 2.0
contour_radius = 1.5
BASE = 4.0
NB = 16
ROWS = 2 * NB
NZ = 4
NX = 16
WIDE = (-2, -1, 0, 1, 2, 3)
UPPER = [(0, k) for k in (-2, -1, 0, 1, 2)] + [(1, k) for k in (-1, 0, 1)] + [(2, 0)]
LOWER = [(3, k) for k in (-1, 0, 1, 2)] + [(2, k) for k in (0, 1)]
UPPER_POT = [(0, -1), (0, 0), (0, 1), (1, 0)]
LOWER_POT = [(3, 0), (3, 1)]
PHASES = (("core", "y"), ("x", "zlo", "zhi"))
POLE = ("x", "zlo", "core")
SLAB = ("y", "zhi")


def own_row():
    return lax.axis_index(POLE)


def gather_rows(row_ref, vectors, potential, own, up, down, sems):
    row = row_ref[0]
    copies = []
    for z in range(NZ):
        for k in WIDE:
            at = lax.rem(row + (k + NX), NX)
            slot = z * len(WIDE) + k + 2
            copy = pltpu.make_async_copy(vectors.at[:, :, z, at, :], own.at[slot], sems.at[slot])
            copy.start()
            copies.append(copy)
    for copy in copies:
        copy.wait()

    def send(out, cells, levels):
        for i, (z, k) in enumerate(cells):
            block = own[z * len(WIDE) + k + 2]
            out[pl.ds(i * ROWS, ROWS), :] = block.reshape(ROWS, 128)
        for i, (z, k) in enumerate(levels):
            at = lax.rem(row + (k + NX), NX)
            out[pl.ds(len(cells) * ROWS + i, 1), :] = potential[z, pl.ds(at, 1), :]
        rest = 8 - len(levels)
        out[pl.ds(len(cells) * ROWS + len(levels), rest), :] = jnp.zeros((rest, 128), jnp.float32)

    send(down, UPPER, UPPER_POT)
    send(up, LOWER, LOWER_POT)


def krylov_gram(row_ref, own, above, below, potential, packed, fields, stack):
    row = row_ref[0]
    v0, diag = {}, {}
    for z in range(NZ):
        for k in WIDE:
            v0[z, k] = own[z * len(WIDE) + k + 2].reshape(ROWS, 128)
        for k in (-1, 0, 1, 2):
            at = lax.rem(row + (k + NX), NX)
            diag[z, k] = potential[z, pl.ds(at, 1), :] + (3.0 - BASE)
    for i, (z, k) in enumerate(UPPER):
        v0[z + NZ, k] = above[pl.ds(i * ROWS, ROWS), :]
    for i, (z, k) in enumerate(UPPER_POT):
        diag[z + NZ, k] = above[pl.ds(len(UPPER) * ROWS + i, 1), :] + (3.0 - BASE)
    for i, (z, k) in enumerate(LOWER):
        v0[z - NZ, k] = below[pl.ds(i * ROWS, ROWS), :]
    for i, (z, k) in enumerate(LOWER_POT):
        diag[z - NZ, k] = below[pl.ds(len(LOWER) * ROWS + i, 1), :] + (3.0 - BASE)

    def apply(v, z, k):
        here = v[z, k]
        beside = v[z - 1, k] + v[z + 1, k] + (v[z, k - 1] + v[z, k + 1])
        beside = beside + (pltpu.roll(here, 1, 1) + pltpu.roll(here, 127, 1))
        return diag[z, k] * here - 0.5 * beside

    v1, v2 = {}, {}
    for z, k in (
        [(z, 0) for z in range(-1, 6)]
        + [(z, 1) for z in range(-1, 5)]
        + [(z, -1) for z in range(0, 5)]
        + [(z, 2) for z in range(0, 4)]
    ):
        v1[z, k] = apply(v0, z, k)
    for z, k in [(z, 0) for z in range(0, 5)] + [(z, 1) for z in range(0, 4)]:
        v2[z, k] = apply(v1, z, k)
    for z in range(NZ):
        here = v2[z, 0]
        ahead = v2[z + 1, 0] + v2[z, 1] + pltpu.roll(here, 127, 1)
        half = 0.5 * (diag[z, 0] * here - ahead)
        for i, block in enumerate((v0[z, 0], v1[z, 0], here)):
            fields[z, pl.ds(i * ROWS, ROWS), :] = block
            stack[pl.ds(i * ROWS, ROWS), pl.ds(z * 128, 128)] = block
        stack[pl.ds(3 * ROWS, ROWS), pl.ds(z * 128, 128)] = half
    gram = lax.dot_general(
        stack[...],
        stack[...],
        (((1,), (1,)), ((), ())),
        precision=lax.Precision.HIGHEST,
        preferred_element_type=jnp.float32,
    )
    lane = lax.broadcasted_iota(jnp.int32, (NB, 128), 1)
    sub = lax.broadcasted_iota(jnp.int32, (NB, 128), 0)
    result = jnp.zeros((NB, 128), jnp.float32)
    blocks = [[(0, 0)], [(0, 1)], [(1, 1)], [(1, 2)], [(2, 2)], [(2, 3), (3, 2)]]
    for n, parts in enumerate(blocks):
        rr = ri = ir = ii = 0.0
        for i, j in parts:
            top = gram[ROWS * i : ROWS * i + NB, :]
            low = gram[ROWS * i + NB : ROWS * i + ROWS, :]
            first = (NB * n - ROWS * j) % 128
            second = (NB * n - ROWS * j - NB) % 128
            rr = rr + (pltpu.roll(top, first, 1) if first else top)
            ri = ri + (pltpu.roll(top, second, 1) if second else top)
            ir = ir + (pltpu.roll(low, first, 1) if first else low)
            ii = ii + (pltpu.roll(low, second, 1) if second else low)
        col = lane - NB * n
        inside = (col >= 0) & (col < NB)
        result = jnp.where(inside, jnp.where(col >= sub, rr + ii, ri - ir), result)
        on = col == sub
        m_re = jnp.sum(jnp.where(on, rr - ii, 0.0), axis=1, keepdims=True)
        m_im = jnp.sum(jnp.where(on, ri + ir, 0.0), axis=1, keepdims=True)
        result = jnp.where(lane == 6 * NB + 2 * n, m_re, result)
        result = jnp.where(lane == 6 * NB + 2 * n + 1, m_im, result)
    packed[...] = result


def cmul(a, b):
    return (a[0] * b[0] - a[1] * b[1], a[0] * b[1] + a[1] * b[0])


def cadd(a, b):
    return (a[0] + b[0], a[1] + b[1])


def csub(a, b):
    return (a[0] - b[0], a[1] - b[1])


def cdiv(a, b):
    size = b[0] * b[0] + b[1] * b[1]
    return ((a[0] * b[0] + a[1] * b[1]) / size, (a[1] * b[0] - a[0] * b[1]) / size)


def combine(poles, cells, parts, total, fields, filtered, correlation, energy):
    moments = total[...]
    lane = lax.broadcasted_iota(jnp.int32, (NB, 128), 1)
    m = [
        tuple(
            jnp.broadcast_to(moments[:, 6 * NB + 2 * n + c : 6 * NB + 2 * n + c + 1], (NB, 128))
            for c in (0, 1)
        )
        for n in range(6)
    ]
    cosine = jnp.zeros((NB, 128), jnp.float32)
    sine = jnp.zeros((NB, 128), jnp.float32)
    for j in range(poles):
        angle = 2.0 * math.pi / poles * (j + 0.5)
        cosine = jnp.where(lane == j, math.cos(angle), cosine)
        sine = jnp.where(lane == j, math.sin(angle), sine)
    shift = (contour_center + contour_radius * cosine, contour_radius * sine)
    weight = (contour_radius * cosine / poles, contour_radius * sine / poles)
    zeta = (shift[0] - BASE, shift[1])

    def form(p, q):
        sums = {}
        for i, a in enumerate(p):
            for j, b in enumerate(q):
                ab = cmul(a, b)
                sums[i + j] = cadd(sums[i + j], ab) if i + j in sums else ab
        out = None
        for n, s in sums.items():
            term = cmul(s, m[n])
            out = term if out is None else cadd(out, term)
        return out

    def applied(p):
        q = [cmul(zeta, a) for a in p]
        q = [q[0]] + [csub(q[i], p[i - 1]) for i in range(1, len(p))]
        return q + [(-p[-1][0], -p[-1][1])]

    one = (jnp.ones((NB, 128), jnp.float32), jnp.zeros((NB, 128), jnp.float32))
    residual, direction, solution_ = [one], [one], []
    rho = m[0]
    for iteration in range(3):
        q = applied(direction)
        alpha = cdiv(rho, form(direction, q))
        step = [cmul(alpha, d) for d in direction]
        solution_ = [cadd(s, t) for s, t in zip(solution_, step)] + step[len(solution_) :]
        step = [cmul(alpha, d) for d in q]
        residual = [csub(r, t) for r, t in zip(residual, step)] + [
            (-t[0], -t[1]) for t in step[len(residual) :]
        ]
        if iteration < 2:
            rho_new = form(residual, residual)
            beta = cdiv(rho_new, rho)
            step = [cmul(beta, d) for d in direction]
            direction = [cadd(r, t) for r, t in zip(residual, step)] + residual[len(step) :]
            rho = rho_new
    image = []
    for k in range(4):
        term = residual[k]
        if k < 3:
            term = cadd(term, cmul(shift, solution_[k]))
        if k == 0:
            term = (term[0] - 1.0, term[1])
        image.append(term)

    def over_poles(term):
        term = cmul(weight, term)
        return tuple(
            jnp.sum(jnp.where(lane < poles, t, 0.0), axis=1, keepdims=True) for t in term
        )

    coef = [over_poles(s) for s in solution_]
    coef_image = [over_poles(s) for s in image]
    for z in range(NZ):
        re = im = 0.0
        for k in range(3):
            v_re = fields[z, pl.ds(k * ROWS, NB), :]
            v_im = fields[z, pl.ds(k * ROWS + NB, NB), :]
            re = re + (coef[k][0] * v_re - coef[k][1] * v_im)
            im = im + (coef[k][0] * v_im + coef[k][1] * v_re)
        filtered[0, :, z, :] = re
        filtered[1, :, z, :] = im

    a = lax.broadcasted_iota(jnp.int32, (NB, NB), 0)
    b = lax.broadcasted_iota(jnp.int32, (NB, NB), 1)
    flipped = lax.dot_general(
        moments,
        jnp.where(a == b, 1.0, 0.0),
        (((0,), (0,)), ((), ())),
        precision=lax.Precision.HIGHEST,
        preferred_element_type=jnp.float32,
    )
    inner = []
    for n in range(6):
        here = moments[:, NB * n : NB * n + NB]
        there = flipped[NB * n : NB * n + NB, :]
        inner.append(
            (
                jnp.where(b >= a, here, there),
                jnp.where(b < a, here, jnp.where(b > a, -there, 0.0)),
            )
        )

    def as_row(c):
        return tuple(
            jnp.sum(jnp.where(a == b, jnp.broadcast_to(t, (NB, NB)), 0.0), axis=0, keepdims=True)
            for t in c
        )

    def product(right, out):
        rows = [as_row(c) for c in right]
        result = None
        for k in range(3):
            part = None
            for l, r in enumerate(rows):
                term = cmul(r, inner[k + l])
                part = term if part is None else cadd(part, term)
            term = cmul((coef[k][0], -coef[k][1]), part)
            result = term if result is None else cadd(result, term)
        out[0] = result[0] * (1.0 / cells)
        out[1] = result[1] * (1.0 / cells)

    product(coef, correlation)
    product(coef_image, energy)


def on_device(vectors, potential):
    f32 = jnp.float32
    vmem = pl.BlockSpec(memory_space=pltpu.VMEM)
    smem = pl.BlockSpec(memory_space=pltpu.SMEM)
    row = own_row().reshape(1).astype(jnp.int32)
    slots = NZ * len(WIDE)
    own, up, down = pl.pallas_call(
        gather_rows,
        in_specs=[smem, pl.BlockSpec(memory_space=pl.ANY), vmem],
        out_specs=[vmem] * 3,
        out_shape=[
            jax.ShapeDtypeStruct((slots, 2, NB, 128), f32),
            jax.ShapeDtypeStruct((len(LOWER) * ROWS + 8, 128), f32),
            jax.ShapeDtypeStruct((len(UPPER) * ROWS + 8, 128), f32),
        ],
        scratch_shapes=[pltpu.SemaphoreType.DMA((slots,))],
        name="gather_rows",
    )(row, vectors, potential)
    slabs = lax.axis_size(SLAB)
    ahead = [(i, (i + 1) % slabs) for i in range(slabs)]
    back = [(i, (i - 1) % slabs) for i in range(slabs)]
    above = lax.ppermute(down, SLAB, back)
    below = lax.ppermute(up, SLAB, ahead)
    packed, fields = pl.pallas_call(
        krylov_gram,
        in_specs=[smem] + [vmem] * 4,
        out_specs=[vmem] * 2,
        out_shape=[
            jax.ShapeDtypeStruct((NB, 128), f32),
            jax.ShapeDtypeStruct((NZ, 3 * ROWS, 128), f32),
        ],
        scratch_shapes=[pltpu.VMEM((4 * ROWS, NZ * 128), f32)],
        name="krylov_gram",
    )(row, own, above, below, potential)
    for axes in PHASES:
        count = lax.axis_size(axes)
        shared = jnp.broadcast_to(packed[None], (count, NB, 128))
        packed = jnp.sum(lax.all_to_all(shared, axes, 0, 0), axis=0)
    cells = NZ * slabs * NX * 128
    filtered, correlation, energy = pl.pallas_call(
        functools.partial(combine, lax.axis_size(POLE), cells, None),
        in_specs=[vmem] * 2,
        out_specs=[vmem] * 3,
        out_shape=[
            jax.ShapeDtypeStruct((2, NB, NZ, 128), f32),
            jax.ShapeDtypeStruct((2, NB, NB), f32),
            jax.ShapeDtypeStruct((2, NB, NB), f32),
        ],
        name="combine",
    )(packed, fields)
    return filtered[:, :, :, None, :], correlation, energy


def solution(mesh):
    fine = Mesh(mesh.devices.reshape(4, 2, 2, 8, 4), POLE + SLAB)
    in_specs = (P(None, None, SLAB, None, None), P(SLAB, None, None))
    out_specs = (P(None, None, SLAB, POLE, None), P(), P())
    return jax.shard_map(
        on_device, mesh=fine, in_specs=in_specs, out_specs=out_specs, check_vma=False
    )
```

time: 802 us -> 66 us (0.08)
  the two profiles are of different devices: /device:TPU:32 before, /device:TPU:8 now
where the time goes in v1:
time: 66 us; the launch traced here: 65.5 us
  blocking collectives  32.9 us (50%)
  starting transfers between devices  12.7 us (19%)
  waiting for transfers between devices  9.72 us (15%)
  Pallas kernels  7.4 us (11%)
  local copies, waits for them, and re-layouts  1.44 us (2%)
  between operations  0.68 us (1%)
    all_to_all x2, blocking collectives, on_device(): packed = jnp.sum(lax.all_to_all(shared, axes, 0, 0), axis=0)  32.9 us
    ppermute x1, starting transfers between devices, on_device(): above = lax.ppermute(down, SLAB, back)  10.8 us
    ppermute x1, waiting for transfers between devices, on_device(): below = lax.ppermute(up, SLAB, ahead)  9.72 us
    pallas_call x1, Pallas kernels, on_device(): pl.pallas_call(gather_rows, in_specs=[smem, pl.BlockSpec(memory_space=pl....  2.79 us
    pallas_call x1, Pallas kernels, on_device(): pl.pallas_call(krylov_gram, in_specs=[smem] + [vmem] * 4, out_specs=[vmem...  2.56 us
    pallas_call x1, Pallas kernels, on_device(): pl.pallas_call(functools.partial(combine, lax.axis_size(POLE), cells, Non...  2.06 us
    ppermute x1, starting transfers between devices, on_device(): below = lax.ppermute(up, SLAB, ahead)  1.92 us
  transfers between devices with their start and end apart: 2, of which 1 were waited for; matrix products, arithmetic and copies ran while one was open for 0% of the time, Pallas kernels for 0%

profile of v1, /device:TPU:8, one launch (start us, length us, event | category | flops | bytes accessed | tf_op | source)
XLA Modules:
  0.0 65.5 jit_solution(9614715821193197003)
XLA Ops:
  0.6 2.8 %gather_rows.1 = (f32[24,2,16,128]{3,2,1,0:T(8,128)}, f32[200,128]{1,0:T(8,128)}, f32[296,128]{1,0:T(8,128)}) custom-call(s32[1]{0:T(128)} %bitcast.row_ref, f32[2,16,4,16,128]{4,3,2,1,0:T(8,128)} %vectors.1, f32[4,16,128]{2,1,0:T(8,128)} %potential.3), custom_call_target="tpu_custom_call" | custom-call | tf_op jit(solution)/shard_map/gather_rows/pallas_call | solution.py:283
  3.4 10.8 %collective-permute-start = (f32[296,128]{1,0:T(8,128)}, f32[296,128]{1,0:T(8,128)S(1)}, u32[]{:S(2)}, u32[]{:S(2)}) collective-permute-start(f32[296,128]{1,0:T(8,128)} %get-tuple-element.12), channel_id=1, source_target_pairs={{0,31},{1,0},{2,1},{3,2},{4,3},{5,4},{6,5},{7,6},{8,7},{9,8},{10,9... | collective-permute-start | bytes 454664 | tf_op jit(solution)/shard_map/ppermute | solution.py:298
  14.3 1.9 %collective-permute-start.1 = (f32[200,128]{1,0:T(8,128)}, f32[200,128]{1,0:T(8,128)S(1)}, u32[]{:S(2)}, u32[]{:S(2)}) collective-permute-start(f32[200,128]{1,0:T(8,128)} %get-tuple-element.13), channel_id=1, source_target_pairs={{0,1},{1,2},{2,3},{3,4},{4,5},{5,6},{6,7},{7,8},{8,9},{9,10},{10,1... | collective-permute-start | bytes 307208 | tf_op jit(solution)/shard_map/ppermute | solution.py:299
  16.2 9.7 %collective-permute-done.1.below = f32[200,128]{1,0:T(8,128)S(1)} collective-permute-done((f32[200,128]{1,0:T(8,128)}, f32[200,128]{1,0:T(8,128)S(1)}, u32[]{:S(2)}, u32[]{:S(2)}) %collective-permute-start.1) | collective-permute-done | bytes 102432 | tf_op jit(solution)/shard_map/ppermute | solution.py:299
  25.9 0.0 copy-start.1
  25.9 0.0 collective-permute-done.above
  25.9 0.0 copy-start
  25.9 0.6 copy-done.1
  26.6 0.1 copy-done
  26.6 2.6 %krylov_gram.1 = (f32[16,128]{1,0:T(8,128)}, f32[4,96,128]{2,1,0:T(8,128)}) custom-call(s32[1]{0:T(128)} %bitcast.row_ref, f32[24,2,16,128]{3,2,1,0:T(8,128)} %get-tuple-element.11.own, f32[296,128]{1,0:T(8,128)} %copy-done, f32[200,128]{1,0:T(8,128)} %copy-done.1, f32[4,16,128]{2,1,0:T(8,128)} %potential.3), custom_call_target="tpu_custom_call" | custom-call | tf_op jit(solution)/shard_map/krylov_gram/pallas_call | solution.py:300
  29.2 0.7 %broadcast_in_dim.6 = f32[16,16,128]{2,1,0:T(8,128)S(1)} broadcast(f32[16,128]{1,0:T(8,128)} %get-tuple-element.14), dimensions={1,2} | broadcast | bytes 139264 | tf_op jit(solution)/shard_map/broadcast_in_dim | solution.py:313
  29.9 16.8 %all_to_all.10 = f32[16,16,128]{2,1,0:T(8,128)S(1)} all-to-all(f32[16,16,128]{2,1,0:T(8,128)S(1)} %broadcast_in_dim.6), channel_id=1, replica_groups=mesh['x'=4,'zlo'=2,'core'=2,'y'=8,'zhi'=4] {'core','y'}, dimensions={0} | all-to-all | bytes 262144 | tf_op jit(solution)/shard_map/all_to_all | solution.py:314
  46.7 16.1 %all_to_all.11 = f32[32,16,128]{2,1,0:T(8,128)S(1)} all-to-all(f32[32,16,128]{2,1,0:T(8,128)S(1)} %broadcast_in_dim.7), channel_id=1, replica_groups=mesh['x'=4,'zlo'=2,'core'=2,'y'=8,'zhi'=4] {'x','zlo','zhi'}, dimensions={0} | all-to-all | bytes 524288 | tf_op jit(solution)/shard_map/all_to_all | solution.py:314
  62.8 0.6 reduce_sum.19.total
  63.5 2.1 %combine.1 = (f32[2,16,4,128]{3,2,1,0:T(4,128)}, f32[2,16,16]{2,1,0:T(8,128)}, f32[2,16,16]{2,1,0:T(8,128)}) custom-call(f32[16,128]{1,0:T(8,128)} %reduce_sum.19.total, f32[4,96,128]{2,1,0:T(8,128)} %get-tuple-element.15.fields), custom_call_target="tpu_custom_call" | custom-call | tf_op jit(solution)/shard_map/combine/pallas_call | solution.py:316
  (2 shorter events, 0.0 us)
Async XLA Ops:
  3.4 22.5 %collective-permute-start = (f32[296,128]{1,0:T(8,128)}, f32[296,128]{1,0:T(8,128)S(1)}, u32[]{:S(2)}, u32[]{:S(2)}) collective-permute-start(f32[296,128]{1,0:T(8,128)} %get-tuple-element.12), channel_id=1, source_target_pairs={{0,31},{1,0},{2,1},{3,2},{4,3},{5,4},{6,5},{7,6},{8,7},{9,8},{10,9... | collective-permute-start | bytes 454664 | tf_op jit(solution)/shard_map/ppermute | solution.py:298
  14.3 11.6 %collective-permute-start.1 = (f32[200,128]{1,0:T(8,128)}, f32[200,128]{1,0:T(8,128)S(1)}, u32[]{:S(2)}, u32[]{:S(2)}) collective-permute-start(f32[200,128]{1,0:T(8,128)} %get-tuple-element.13), channel_id=1, source_target_pairs={{0,1},{1,2},{2,3},{3,4},{4,5},{5,6},{6,7},{7,8},{8,9},{9,10},{10,1... | collective-permute-start | bytes 307208 | tf_op jit(solution)/shard_map/ppermute | solution.py:299
  25.9 0.6 copy-start.1
  25.9 0.7 %copy-start = (f32[296,128]{1,0:T(8,128)}, f32[296,128]{1,0:T(8,128)S(1)}, u32[]{:S(2)}) copy-start(f32[296,128]{1,0:T(8,128)S(1)} %collective-permute-done.above) | copy-start | bytes 454660

commit v2 on v1

--- a/solution.py
+++ b/solution.py
@@ -17,11 +17,11 @@
 NZ = 4
 NX = 16
 WIDE = (-2, -1, 0, 1, 2, 3)
-UPPER = [(0, k) for k in (-2, -1, 0, 1, 2)] + [(1, k) for k in (-1, 0, 1)] + [(2, 0)]
-LOWER = [(3, k) for k in (-1, 0, 1, 2)] + [(2, k) for k in (0, 1)]
-UPPER_POT = [(0, -1), (0, 0), (0, 1), (1, 0)]
-LOWER_POT = [(3, 0), (3, 1)]
-PHASES = (("core", "y"), ("x", "zlo", "zhi"))
+LOWER = [(3, k) for k in (-2, -1, 0, 1, 2)] + [(2, k) for k in (-1, 0, 1)] + [(1, 0)]
+UPPER = [(0, k) for k in (-1, 0, 1, 2)] + [(1, k) for k in (0, 1)]
+LOWER_POT = [(3, -1), (3, 0), (3, 1), (2, 0)]
+UPPER_POT = [(0, 0), (0, 1)]
+PHASES = (("x", "zlo", "zhi"), ("core", "y"))
 POLE = ("x", "zlo", "core")
 SLAB = ("y", "zhi")
 
@@ -30,16 +30,18 @@
     return lax.axis_index(POLE)
 
 
-def gather_rows(row_ref, vectors, potential, own, up, down, sems):
+def gather_rows(row_ref, vectors, potential, own, up, down, levels_out, sems):
     row = row_ref[0]
-    copies = []
-    for z in range(NZ):
+    copies = [pltpu.make_async_copy(potential, levels_out, sems.at[NZ * len(WIDE)])]
+    for z in (3, 0, 2, 1):
         for k in WIDE:
             at = lax.rem(row + (k + NX), NX)
             slot = z * len(WIDE) + k + 2
-            copy = pltpu.make_async_copy(vectors.at[:, :, z, at, :], own.at[slot], sems.at[slot])
-            copy.start()
-            copies.append(copy)
+            copies.append(
+                pltpu.make_async_copy(vectors.at[:, :, z, at, :], own.at[slot], sems.at[slot])
+            )
+    for copy in copies:
+        copy.start()
     for copy in copies:
         copy.wait()
 
@@ -49,7 +51,7 @@
             out[pl.ds(i * ROWS, ROWS), :] = block.reshape(ROWS, 128)
         for i, (z, k) in enumerate(levels):
             at = lax.rem(row + (k + NX), NX)
-            out[pl.ds(len(cells) * ROWS + i, 1), :] = potential[z, pl.ds(at, 1), :]
+            out[pl.ds(len(cells) * ROWS + i, 1), :] = levels_out[z, pl.ds(at, 1), :]
         rest = 8 - len(levels)
         out[pl.ds(len(cells) * ROWS + len(levels), rest), :] = jnp.zeros((rest, 128), jnp.float32)
 
@@ -83,17 +85,17 @@
 
     v1, v2 = {}, {}
     for z, k in (
-        [(z, 0) for z in range(-1, 6)]
+        [(z, 0) for z in range(-2, 5)]
         + [(z, 1) for z in range(-1, 5)]
-        + [(z, -1) for z in range(0, 5)]
+        + [(z, -1) for z in range(-1, 4)]
         + [(z, 2) for z in range(0, 4)]
     ):
         v1[z, k] = apply(v0, z, k)
-    for z, k in [(z, 0) for z in range(0, 5)] + [(z, 1) for z in range(0, 4)]:
+    for z, k in [(z, 0) for z in range(-1, 4)] + [(z, 1) for z in range(0, 4)]:
         v2[z, k] = apply(v1, z, k)
     for z in range(NZ):
         here = v2[z, 0]
-        ahead = v2[z + 1, 0] + v2[z, 1] + pltpu.roll(here, 127, 1)
+        ahead = v2[z - 1, 0] + v2[z, 1] + pltpu.roll(here, 127, 1)
         half = 0.5 * (diag[z, 0] * here - ahead)
         for i, block in enumerate((v0[z, 0], v1[z, 0], here)):
             fields[z, pl.ds(i * ROWS, ROWS), :] = block
@@ -278,25 +280,28 @@
     f32 = jnp.float32
     vmem = pl.BlockSpec(memory_space=pltpu.VMEM)
     smem = pl.BlockSpec(memory_space=pltpu.SMEM)
+    vectors = pltpu.with_memory_space_constraint(vectors, pltpu.HBM)
+    potential = pltpu.with_memory_space_constraint(potential, pltpu.HBM)
     row = own_row().reshape(1).astype(jnp.int32)
     slots = NZ * len(WIDE)
-    own, up, down = pl.pallas_call(
+    own, up, down, levels = pl.pallas_call(
         gather_rows,
-        in_specs=[smem, pl.BlockSpec(memory_space=pl.ANY), vmem],
-        out_specs=[vmem] * 3,
+        in_specs=[smem] + [pl.BlockSpec(memory_space=pltpu.HBM)] * 2,
+        out_specs=[vmem] * 4,
         out_shape=[
             jax.ShapeDtypeStruct((slots, 2, NB, 128), f32),
             jax.ShapeDtypeStruct((len(LOWER) * ROWS + 8, 128), f32),
             jax.ShapeDtypeStruct((len(UPPER) * ROWS + 8, 128), f32),
+            jax.ShapeDtypeStruct(potential.shape, f32),
         ],
-        scratch_shapes=[pltpu.SemaphoreType.DMA((slots,))],
-        name="gather_rows",
+        scratch_shapes=[pltpu.SemaphoreType.DMA((slots + 1,))],
+        name="gather_rows", compiler_params=pltpu.CompilerParams(vmem_limit_bytes=8 << 20),
     )(row, vectors, potential)
     slabs = lax.axis_size(SLAB)
     ahead = [(i, (i + 1) % slabs) for i in range(slabs)]
     back = [(i, (i - 1) % slabs) for i in range(slabs)]
+    below = lax.ppermute(up, SLAB, ahead)
     above = lax.ppermute(down, SLAB, back)
-    below = lax.ppermute(up, SLAB, ahead)
     packed, fields = pl.pallas_call(
         krylov_gram,
         in_specs=[smem] + [vmem] * 4,
@@ -306,8 +311,8 @@
             jax.ShapeDtypeStruct((NZ, 3 * ROWS, 128), f32),
         ],
         scratch_shapes=[pltpu.VMEM((4 * ROWS, NZ * 128), f32)],
-        name="krylov_gram",
-    )(row, own, above, below, potential)
+        name="krylov_gram", compiler_params=pltpu.CompilerParams(vmem_limit_bytes=8 << 20),
+    )(row, own, above, below, levels)
     for axes in PHASES:
         count = lax.axis_size(axes)
         shared = jnp.broadcast_to(packed[None], (count, NB, 128))
@@ -322,7 +327,7 @@
             jax.ShapeDtypeStruct((2, NB, NB), f32),
             jax.ShapeDtypeStruct((2, NB, NB), f32),
         ],
-        name="combine",
+        name="combine", compiler_params=pltpu.CompilerParams(vmem_limit_bytes=8 << 20),
     )(packed, fields)
     return filtered[:, :, :, None, :], correlation, energy
 

time: 66 us -> 57.7 us (0.87)
  the two profiles are of different devices: /device:TPU:8 before, /device:TPU:1 now
where the time goes in v2:
time: 57.7 us; the launch traced here: 57.4 us
  blocking collectives  32.9 us (57%)
  starting transfers between devices  16.3 us (28%)
  waiting for transfers between devices  4.15 us (7%)
  Pallas kernels  3.21 us (6%)
  between operations  0.69 us (1%)
    all_to_all x2, blocking collectives, on_device(): packed = jnp.sum(lax.all_to_all(shared, axes, 0, 0), axis=0)  32.9 us
    ppermute x1, starting transfers between devices, on_device(): above = lax.ppermute(down, SLAB, back)  9.67 us
    ppermute x1, starting transfers between devices, on_device(): below = lax.ppermute(up, SLAB, ahead)  6.64 us
    ppermute x1, waiting for transfers between devices, on_device(): below = lax.ppermute(up, SLAB, ahead)  2.21 us
    ppermute x1, waiting for transfers between devices, on_device(): above = lax.ppermute(down, SLAB, back)  1.94 us
    pallas_call x1, Pallas kernels, on_device(): pl.pallas_call(gather_rows, in_specs=[smem] + [pl.BlockSpec(memory_space=...  1.23 us
  transfers between devices with their start and end apart: 2, of which 2 were waited for; matrix products, arithmetic and copies ran while one was open for 0% of the time, Pallas kernels for 0%

profile of v2, /device:TPU:1, one launch (start us, length us, event | category | flops | bytes accessed | tf_op | source)
XLA Modules:
  0.0 57.4 jit_solution(17999213766908591397)
XLA Ops:
  0.6 1.2 %gather_rows.1 = (f32[24,2,16,128]{3,2,1,0:T(8,128)S(1)}, f32[296,128]{1,0:T(8,128)S(1)}, f32[200,128]{1,0:T(8,128)S(1)}, f32[4,16,128]{2,1,0:T(8,128)S(1)}) custom-call(s32[1]{0:T(128)} %bitcast.row_ref, f32[2,16,4,16,128]{4,3,2,1,0:T(8,128)} %vectors.1, f32[4,16,128]{2,1,0:T(8,128)} %potential.1), custom_call_target="tpu_custom_call" | custom-call | tf_op jit(solution)/shard_map/gather_rows/pallas_call | solution.py:287
  1.9 6.6 %collective-permute-start.1 = (f32[296,128]{1,0:T(8,128)S(1)}, f32[296,128]{1,0:T(8,128)S(1)}, u32[]{:S(2)}, u32[]{:S(2)}) collective-permute-start(f32[296,128]{1,0:T(8,128)S(1)} %get-tuple-element.14), channel_id=1, source_target_pairs={{0,1},{1,2},{2,3},{3,4},{4,5},{5,6},{6,7},{7,8},{8,9},{9,10},{10,1... | collective-permute-start | bytes 454664 | tf_op jit(solution)/shard_map/ppermute | solution.py:303
  8.5 9.7 %collective-permute-start = (f32[200,128]{1,0:T(8,128)S(1)}, f32[200,128]{1,0:T(8,128)S(1)}, u32[]{:S(2)}, u32[]{:S(2)}) collective-permute-start(f32[200,128]{1,0:T(8,128)S(1)} %get-tuple-element.13), channel_id=1, source_target_pairs={{0,31},{1,0},{2,1},{3,2},{4,3},{5,4},{6,5},{7,6},{8,7},{9,8},{10,9... | collective-permute-start | bytes 307208 | tf_op jit(solution)/shard_map/ppermute | solution.py:304
  18.2 1.9 %collective-permute-done.above = f32[200,128]{1,0:T(8,128)S(1)} collective-permute-done((f32[200,128]{1,0:T(8,128)S(1)}, f32[200,128]{1,0:T(8,128)S(1)}, u32[]{:S(2)}, u32[]{:S(2)}) %collective-permute-start) | collective-permute-done | bytes 102432 | tf_op jit(solution)/shard_map/ppermute | solution.py:304
  20.1 2.2 %collective-permute-done.1.below = f32[296,128]{1,0:T(8,128)S(1)} collective-permute-done((f32[296,128]{1,0:T(8,128)S(1)}, f32[296,128]{1,0:T(8,128)S(1)}, u32[]{:S(2)}, u32[]{:S(2)}) %collective-permute-start.1) | collective-permute-done | bytes 151584 | tf_op jit(solution)/shard_map/ppermute | solution.py:303
  22.4 0.9 %krylov_gram.1 = (f32[16,128]{1,0:T(8,128)S(1)}, f32[4,96,128]{2,1,0:T(8,128)S(1)}) custom-call(s32[1]{0:T(128)} %bitcast.row_ref, f32[24,2,16,128]{3,2,1,0:T(8,128)S(1)} %get-tuple-element.12.own, f32[200,128]{1,0:T(8,128)S(1)} %collective-permute-done.above, f32[296,128]{1,0:T(8,128)S(1)} %collective-permute-done.1.below, ...), custom_call_target="tpu_custom_call" | custom-call | tf_op jit(solution)/shard_map/krylov_gram/pallas_call | solution.py:305
  23.3 15.4 %all_to_all.10 = f32[32,16,128]{2,1,0:T(8,128)S(1)} all-to-all(f32[32,16,128]{2,1,0:T(8,128)S(1)} %broadcast_in_dim.6), channel_id=1, replica_groups=mesh['x'=4,'zlo'=2,'core'=2,'y'=8,'zhi'=4] {'x','zlo','zhi'}, dimensions={0} | all-to-all | bytes 524288 | tf_op jit(solution)/shard_map/all_to_all | solution.py:319
  38.7 17.5 %all_to_all.11 = f32[16,16,128]{2,1,0:T(8,128)S(1)} all-to-all(f32[16,16,128]{2,1,0:T(8,128)S(1)} %broadcast_in_dim.7), channel_id=1, replica_groups=mesh['x'=4,'zlo'=2,'core'=2,'y'=8,'zhi'=4] {'core','y'}, dimensions={0} | all-to-all | bytes 262144 | tf_op jit(solution)/shard_map/all_to_all | solution.py:319
  56.2 1.1 %combine.1 = (f32[2,16,4,128]{3,2,1,0:T(4,128)}, f32[2,16,16]{2,1,0:T(8,128)}, f32[2,16,16]{2,1,0:T(8,128)}) custom-call(f32[16,128]{1,0:T(8,128)S(1)} %reduce_sum.19.total, f32[4,96,128]{2,1,0:T(8,128)S(1)} %get-tuple-element.17.fields), custom_call_target="tpu_custom_call" | custom-call | tf_op jit(solution)/shard_map/combine/pallas_call | solution.py:321
  (4 shorter events, 0.1 us)
Async XLA Ops:
  1.9 20.5 %collective-permute-start.1 = (f32[296,128]{1,0:T(8,128)S(1)}, f32[296,128]{1,0:T(8,128)S(1)}, u32[]{:S(2)}, u32[]{:S(2)}) collective-permute-start(f32[296,128]{1,0:T(8,128)S(1)} %get-tuple-element.14), channel_id=1, source_target_pairs={{0,1},{1,2},{2,3},{3,4},{4,5},{5,6},{6,7},{7,8},{8,9},{9,10},{10,1... | collective-permute-start | bytes 454664 | tf_op jit(solution)/shard_map/ppermute | solution.py:303
  8.5 11.6 %collective-permute-start = (f32[200,128]{1,0:T(8,128)S(1)}, f32[200,128]{1,0:T(8,128)S(1)}, u32[]{:S(2)}, u32[]{:S(2)}) collective-permute-start(f32[200,128]{1,0:T(8,128)S(1)} %get-tuple-element.13), channel_id=1, source_target_pairs={{0,31},{1,0},{2,1},{3,2},{4,3},{5,4},{6,5},{7,6},{8,7},{9,8},{10,9... | collective-permute-start | bytes 307208 | tf_op jit(solution)/shard_map/ppermute | solution.py:304

commit v3 on v2

--- a/solution.py
+++ b/solution.py
@@ -16,11 +16,8 @@
 ROWS = 2 * NB
 NZ = 4
 NX = 16
-WIDE = (-2, -1, 0, 1, 2, 3)
-LOWER = [(3, k) for k in (-2, -1, 0, 1, 2)] + [(2, k) for k in (-1, 0, 1)] + [(1, 0)]
-UPPER = [(0, k) for k in (-1, 0, 1, 2)] + [(1, k) for k in (0, 1)]
-LOWER_POT = [(3, -1), (3, 0), (3, 1), (2, 0)]
-UPPER_POT = [(0, 0), (0, 1)]
+EDGE = {3: (-2, -1, 0, 1, 2), 2: (-1, 0, 1), 1: (0, 1), 0: (-1, 0, 1, 2)}
+WIDE = {z: (-2, -1, 0, 1, 2, 3) for z in (0, 1, 2, 3)}
 PHASES = (("x", "zlo", "zhi"), ("core", "y"))
 POLE = ("x", "zlo", "core")
 SLAB = ("y", "zhi")
@@ -30,77 +27,125 @@
     return lax.axis_index(POLE)
 
 
-def gather_rows(row_ref, vectors, potential, own, up, down, levels_out, sems):
+def fetch(row, vectors, rows, buffer, sems):
+    copies, slots = [], {}
+    for z in rows:
+        for k in rows[z]:
+            at = lax.rem(row + (k + NX), NX)
+            slot = slots[z, k] = len(slots)
+            copies.append(
+                pltpu.make_async_copy(vectors.at[:, :, z, at, :], buffer.at[slot], sems.at[slot])
+            )
+            copies[-1].start()
+    return copies, slots
+
+
+def turned(v):
+    return pltpu.roll(v, 1, 1) + pltpu.roll(v, 127, 1)
+
+
+class Slab:
+    def __init__(self, row, levels):
+        self.row, self.levels, self.diagonals = row, levels, {}
+
+    def diagonal(self, z, k):
+        if (z, k) not in self.diagonals:
+            at = lax.rem(self.row + (k + NX), NX)
+            self.diagonals[z, k] = self.levels[z, pl.ds(at, 1), :] + (3.0 - BASE)
+        return self.diagonals[z, k]
+
+    def apply(self, v, z, k):
+        beside = turned(v(z, k)) + (v(z, k - 1) + v(z, k + 1))
+        if z > 0:
+            beside = beside + v(z - 1, k)
+        if z < NZ - 1:
+            beside = beside + v(z + 1, k)
+        return self.diagonal(z, k) * v(z, k) - 0.5 * beside
+
+
+def slab_edges(row_ref, vectors, potential, up, down, buffer, levels, sems):
     row = row_ref[0]
-    copies = [pltpu.make_async_copy(potential, levels_out, sems.at[NZ * len(WIDE)])]
-    for z in (3, 0, 2, 1):
-        for k in WIDE:
-            at = lax.rem(row + (k + NX), NX)
-            slot = z * len(WIDE) + k + 2
-            copies.append(
-                pltpu.make_async_copy(vectors.at[:, :, z, at, :], own.at[slot], sems.at[slot])
-            )
-    for copy in copies:
-        copy.start()
-    for copy in copies:
+    level_copy = pltpu.make_async_copy(potential, levels, sems.at[sum(map(len, EDGE.values()))])
+    level_copy.start()
+    copies, slots = fetch(row, vectors, EDGE, buffer, sems)
+    for copy in [level_copy] + copies:
         copy.wait()
-
-    def send(out, cells, levels):
-        for i, (z, k) in enumerate(cells):
-            block = own[z * len(WIDE) + k + 2]
-            out[pl.ds(i * ROWS, ROWS), :] = block.reshape(ROWS, 128)
-        for i, (z, k) in enumerate(levels):
-            at = lax.rem(row + (k + NX), NX)
-            out[pl.ds(len(cells) * ROWS + i, 1), :] = levels_out[z, pl.ds(at, 1), :]
-        rest = 8 - len(levels)
-        out[pl.ds(len(cells) * ROWS + len(levels), rest), :] = jnp.zeros((rest, 128), jnp.float32)
-
-    send(down, UPPER, UPPER_POT)
-    send(up, LOWER, LOWER_POT)
-
-
-def krylov_gram(row_ref, own, above, below, potential, packed, fields, stack):
+    slab = Slab(row, levels)
+
+    def field(z, k):
+        return buffer[slots[z, k]].reshape(ROWS, 128)
+
+    def into_next(z, inner, k):
+        around = turned(field(z, k)) + (field(z, k - 1) + field(z, k + 1))
+        return 0.5 * (around - slab.diagonal(z, k) * field(z, k)) + 0.25 * field(inner, k)
+
+    first = {}
+    for z, k in [(2, 0), (3, -1), (3, 0), (3, 1)]:
+        first[z, k] = slab.apply(field, z, k)
+    second = slab.apply(lambda z, k: first[z, k], 3, 0) + 0.25 * field(3, 0)
+    out = [field(3, 0), field(3, 1), into_next(3, 2, 0), into_next(3, 2, 1), second]
+    for i, block in enumerate(out):
+        up[pl.ds(i * ROWS, ROWS), :] = block
+    up[pl.ds(len(out) * ROWS, 8), :] = jnp.broadcast_to(slab.diagonal(3, 0), (8, 128))
+    out = [field(0, 0), field(0, 1), into_next(0, 1, 0), into_next(0, 1, 1)]
+    for i, block in enumerate(out):
+        down[pl.ds(i * ROWS, ROWS), :] = block
+
+
+def slab_fields(row_ref, vectors, potential, inside, diagonals, buffer, levels, sems):
     row = row_ref[0]
-    v0, diag = {}, {}
-    for z in range(NZ):
-        for k in WIDE:
-            v0[z, k] = own[z * len(WIDE) + k + 2].reshape(ROWS, 128)
+    level_copy = pltpu.make_async_copy(potential, levels, sems.at[sum(map(len, WIDE.values()))])
+    level_copy.start()
+    copies, slots = fetch(row, vectors, WIDE, buffer, sems)
+    for copy in [level_copy] + copies:
+        copy.wait()
+    slab = Slab(row, levels)
+
+    def field(z, k):
+        return buffer[slots[z, k]].reshape(ROWS, 128)
+
+    first = {}
+    for z in range(NZ):
         for k in (-1, 0, 1, 2):
-            at = lax.rem(row + (k + NX), NX)
-            diag[z, k] = potential[z, pl.ds(at, 1), :] + (3.0 - BASE)
-    for i, (z, k) in enumerate(UPPER):
-        v0[z + NZ, k] = above[pl.ds(i * ROWS, ROWS), :]
-    for i, (z, k) in enumerate(UPPER_POT):
-        diag[z + NZ, k] = above[pl.ds(len(UPPER) * ROWS + i, 1), :] + (3.0 - BASE)
-    for i, (z, k) in enumerate(LOWER):
-        v0[z - NZ, k] = below[pl.ds(i * ROWS, ROWS), :]
-    for i, (z, k) in enumerate(LOWER_POT):
-        diag[z - NZ, k] = below[pl.ds(len(LOWER) * ROWS + i, 1), :] + (3.0 - BASE)
-
-    def apply(v, z, k):
-        here = v[z, k]
-        beside = v[z - 1, k] + v[z + 1, k] + (v[z, k - 1] + v[z, k + 1])
-        beside = beside + (pltpu.roll(here, 1, 1) + pltpu.roll(here, 127, 1))
-        return diag[z, k] * here - 0.5 * beside
+            first[z, k] = slab.apply(field, z, k)
+    for z in range(NZ):
+        inside[z, 0] = field(z, 0)
+        inside[z, 1] = first[z, 0]
+        for k in (0, 1):
+            second = slab.apply(lambda z, k: first[z, k], z, k)
+            if z in (0, NZ - 1):
+                second = second + 0.25 * field(z, k)
+            inside[z, 2 + k] = second
+            diagonals[pl.ds(2 * z + k, 1), :] = slab.diagonal(z, k)
+
+
+def krylov_gram(inside, diagonals, below, above, down, packed, fields, stack):
+    def part(halo, i):
+        return halo[pl.ds(i * ROWS, ROWS), :]
+
+    def level(z, k):
+        return diagonals[pl.ds(2 * z + k, 1), :]
 
     v1, v2 = {}, {}
-    for z, k in (
-        [(z, 0) for z in range(-2, 5)]
-        + [(z, 1) for z in range(-1, 5)]
-        + [(z, -1) for z in range(-1, 4)]
-        + [(z, 2) for z in range(0, 4)]
-    ):
-        v1[z, k] = apply(v0, z, k)
-    for z, k in [(z, 0) for z in range(-1, 4)] + [(z, 1) for z in range(0, 4)]:
-        v2[z, k] = apply(v1, z, k)
+    for z in range(NZ):
+        v1[z] = inside[z, 1]
+        for k in (0, 1):
+            v2[z, k] = inside[z, 2 + k]
+    for z, near, halo in [(0, 1, below), (3, 2, above)]:
+        v1[z] = v1[z] - 0.5 * part(halo, 0)
+        for k in (0, 1):
+            v2[z, k] = v2[z, k] + (part(halo, 2 + k) - 0.5 * (level(z, k) * part(halo, k)))
+            v2[near, k] = v2[near, k] + 0.25 * part(halo, k)
+    lowest = below[pl.ds(5 * ROWS, 1), :]
+    v2[-1, 0] = part(below, 4) + (part(down, 2) - 0.5 * (lowest * part(down, 0)))
     for z in range(NZ):
         here = v2[z, 0]
         ahead = v2[z - 1, 0] + v2[z, 1] + pltpu.roll(here, 127, 1)
-        half = 0.5 * (diag[z, 0] * here - ahead)
-        for i, block in enumerate((v0[z, 0], v1[z, 0], here)):
-            fields[z, pl.ds(i * ROWS, ROWS), :] = block
+        half = 0.5 * (level(z, 0) * here - ahead)
+        fields[z, 0] = v1[z]
+        fields[z, 1] = here
+        for i, block in enumerate((inside[z, 0], v1[z], here, half)):
             stack[pl.ds(i * ROWS, ROWS), pl.ds(z * 128, 128)] = block
-        stack[pl.ds(3 * ROWS, ROWS), pl.ds(z * 128, 128)] = half
     gram = lax.dot_general(
         stack[...],
         stack[...],
@@ -151,7 +196,7 @@
     return ((a[0] * b[0] + a[1] * b[1]) / size, (a[1] * b[0] - a[0] * b[1]) / size)
 
 
-def combine(poles, cells, parts, total, fields, filtered, correlation, energy):
+def combine(poles, cells, total, inside, fields, filtered, correlation, energy):
     moments = total[...]
     lane = lax.broadcasted_iota(jnp.int32, (NB, 128), 1)
     m = [
@@ -226,8 +271,8 @@
     for z in range(NZ):
         re = im = 0.0
         for k in range(3):
-            v_re = fields[z, pl.ds(k * ROWS, NB), :]
-            v_im = fields[z, pl.ds(k * ROWS + NB, NB), :]
+            v = inside[z, 0] if k == 0 else fields[z, k - 1]
+            v_re, v_im = v[:NB], v[NB:]
             re = re + (coef[k][0] * v_re - coef[k][1] * v_im)
             im = im + (coef[k][0] * v_im + coef[k][1] * v_re)
         filtered[0, :, z, :] = re
@@ -276,59 +321,60 @@
     product(coef_image, energy)
 
 
+def call(kernel, out, scratch, *operands, flops=1 << 20):
+    space = {"s": pltpu.SMEM, "h": pltpu.HBM, "v": pltpu.VMEM}
+    return pl.pallas_call(
+        kernel,
+        in_specs=[pl.BlockSpec(memory_space=space[kind]) for kind, _ in operands],
+        out_specs=[pl.BlockSpec(memory_space=pltpu.VMEM)] * len(out),
+        out_shape=[jax.ShapeDtypeStruct(shape, jnp.float32) for shape in out],
+        scratch_shapes=scratch,
+        compiler_params=pltpu.CompilerParams(vmem_limit_bytes=8 << 20),
+        cost_estimate=pl.CostEstimate(flops=flops, bytes_accessed=1 << 19, transcendentals=0),
+        name=getattr(kernel, "__name__", "combine"),
+    )(*[operand for _, operand in operands])
+
+
 def on_device(vectors, potential):
-    f32 = jnp.float32
-    vmem = pl.BlockSpec(memory_space=pltpu.VMEM)
-    smem = pl.BlockSpec(memory_space=pltpu.SMEM)
     vectors = pltpu.with_memory_space_constraint(vectors, pltpu.HBM)
     potential = pltpu.with_memory_space_constraint(potential, pltpu.HBM)
     row = own_row().reshape(1).astype(jnp.int32)
-    slots = NZ * len(WIDE)
-    own, up, down, levels = pl.pallas_call(
-        gather_rows,
-        in_specs=[smem] + [pl.BlockSpec(memory_space=pltpu.HBM)] * 2,
-        out_specs=[vmem] * 4,
-        out_shape=[
-            jax.ShapeDtypeStruct((slots, 2, NB, 128), f32),
-            jax.ShapeDtypeStruct((len(LOWER) * ROWS + 8, 128), f32),
-            jax.ShapeDtypeStruct((len(UPPER) * ROWS + 8, 128), f32),
-            jax.ShapeDtypeStruct(potential.shape, f32),
-        ],
-        scratch_shapes=[pltpu.SemaphoreType.DMA((slots + 1,))],
-        name="gather_rows", compiler_params=pltpu.CompilerParams(vmem_limit_bytes=8 << 20),
-    )(row, vectors, potential)
+
+    def scratch(rows):
+        slots = sum(map(len, rows.values()))
+        return [
+            pltpu.VMEM((slots, 2, NB, 128), jnp.float32),
+            pltpu.VMEM(potential.shape, jnp.float32),
+            pltpu.SemaphoreType.DMA((slots + 1,)),
+        ]
+
+    source = (("s", row), ("h", vectors), ("h", potential))
+    up, down = call(
+        slab_edges, [(5 * ROWS + 8, 128), (4 * ROWS, 128)], scratch(EDGE), *source
+    )
     slabs = lax.axis_size(SLAB)
-    ahead = [(i, (i + 1) % slabs) for i in range(slabs)]
-    back = [(i, (i - 1) % slabs) for i in range(slabs)]
-    below = lax.ppermute(up, SLAB, ahead)
-    above = lax.ppermute(down, SLAB, back)
-    packed, fields = pl.pallas_call(
+    below = lax.ppermute(up, SLAB, [(i, (i + 1) % slabs) for i in range(slabs)])
+    above = lax.ppermute(down, SLAB, [(i, (i - 1) % slabs) for i in range(slabs)])
+    inside, diagonals = call(
+        slab_fields, [(NZ, 4, ROWS, 128), (2 * NZ, 128)], scratch(WIDE), *source
+    )
+    packed, fields = call(
         krylov_gram,
-        in_specs=[smem] + [vmem] * 4,
-        out_specs=[vmem] * 2,
-        out_shape=[
-            jax.ShapeDtypeStruct((NB, 128), f32),
-            jax.ShapeDtypeStruct((NZ, 3 * ROWS, 128), f32),
-        ],
-        scratch_shapes=[pltpu.VMEM((4 * ROWS, NZ * 128), f32)],
-        name="krylov_gram", compiler_params=pltpu.CompilerParams(vmem_limit_bytes=8 << 20),
-    )(row, own, above, below, levels)
+        [(NB, 128), (NZ, 2, ROWS, 128)],
+        [pltpu.VMEM((4 * ROWS, NZ * 128), jnp.float32)],
+        *(("v", a) for a in (inside, diagonals, below, above, down)),
+    )
     for axes in PHASES:
         count = lax.axis_size(axes)
         shared = jnp.broadcast_to(packed[None], (count, NB, 128))
         packed = jnp.sum(lax.all_to_all(shared, axes, 0, 0), axis=0)
     cells = NZ * slabs * NX * 128
-    filtered, correlation, energy = pl.pallas_call(
-        functools.partial(combine, lax.axis_size(POLE), cells, None),
-        in_specs=[vmem] * 2,
-        out_specs=[vmem] * 3,
-        out_shape=[
-            jax.ShapeDtypeStruct((2, NB, NZ, 128), f32),
-            jax.ShapeDtypeStruct((2, NB, NB), f32),
-            jax.ShapeDtypeStruct((2, NB, NB), f32),
-        ],
-        name="combine", compiler_params=pltpu.CompilerParams(vmem_limit_bytes=8 << 20),
-    )(packed, fields)
+    filtered, correlation, energy = call(
+        functools.partial(combine, lax.axis_size(POLE), cells),
+        [(2, NB, NZ, 128), (2, NB, NB), (2, NB, NB)],
+        [],
+        *(("v", a) for a in (packed, inside, fields)),
+    )
     return filtered[:, :, :, None, :], correlation, energy
 
 

time: 57.7 us -> 55.4 us (0.960)
  waiting for transfers between devices: 4.15 us -> 0.01 us
  Pallas kernels: 3.21 us -> 4.39 us
  blocking collectives: 32.9 us -> 33.5 us
    ppermute x2, waiting for transfers between devices: 4.15 us -> 0.01 us  [the longest x1 0.01 us: on_device(): lax.ppermute(down, SLAB, [(i, (i - 1) % slabs) for i in range(slabs)])]
    pallas_call x3 -> x4, Pallas kernels: 3.21 us -> 4.39 us  [call(): pl.pallas_call(kernel, in_specs=[pl.BlockSpec(memory_space=space[kind]) f...]
    all_to_all x2, blocking collectives: 32.9 us -> 33.5 us  [on_device(): packed = jnp.sum(lax.all_to_all(shared, axes, 0, 0), axis=0)]
  transfers between devices with their start and end apart: 2 -> 2, of which waited for: 2 -> 0; matrix products, arithmetic and copies ran while one was open for 0% -> 0% of each run, Pallas kernels for 0% -> 3%
where the time goes in v3:
time: 55.4 us; the launch traced here: 55 us
  blocking collectives  33.5 us (60%)
  starting transfers between devices  16.3 us (29%)
  Pallas kernels  4.39 us (8%)
  between operations  0.72 us (1%)
    all_to_all x2, blocking collectives, on_device(): packed = jnp.sum(lax.all_to_all(shared, axes, 0, 0), axis=0)  33.5 us
    ppermute x1, starting transfers between devices, on_device(): lax.ppermute(down, SLAB, [(i, (i - 1) % slabs) for i in range(slabs)])  9.67 us
    ppermute x1, starting transfers between devices, on_device(): below = lax.ppermute(up, SLAB, [(i, (i + 1) % slabs) for i in range(slabs)])  6.64 us
    pallas_call x4, Pallas kernels, call(): pl.pallas_call(kernel, in_specs=[pl.BlockSpec(memory_space=space[kind]) f...  4.39 us
  transfers between devices with their start and end apart: 2, of which 0 were waited for; matrix products, arithmetic and copies ran while one was open for 0% of the time, Pallas kernels for 3%

profile of v3, /device:TPU:1, one launch (start us, length us, event | category | flops | bytes accessed | tf_op | source)
XLA Modules:
  0.0 55.0 jit_solution(3904322110053669825)
XLA Ops:
  0.6 1.2 %slab_edges.1 = (f32[168,128]{1,0:T(8,128)S(1)}, f32[128,128]{1,0:T(8,128)S(1)}) custom-call(s32[1]{0:T(128)} %bitcast.row_ref, f32[2,16,4,16,128]{4,3,2,1,0:T(8,128)} %vectors.3, f32[4,16,128]{2,1,0:T(8,128)} %potential.3), custom_call_target="tpu_custom_call" | custom-call | flops 1048576 | bytes 524288 | tf_op jit(solution)/shard_map/slab_edges/pallas_call | solution.py:326
  1.8 6.6 %collective-permute-start = (f32[168,128]{1,0:T(8,128)S(1)}, f32[168,128]{1,0:T(8,128)S(1)}, u32[]{:S(2)}, u32[]{:S(2)}) collective-permute-start(f32[168,128]{1,0:T(8,128)S(1)} %get-tuple-element.14), channel_id=1, source_target_pairs={{0,1},{1,2},{2,3},{3,4},{4,5},{5,6},{6,7},{7,8},{8,9},{9,10},{10,1... | collective-permute-start | bytes 258056 | tf_op jit(solution)/shard_map/ppermute | solution.py:356
  8.5 9.7 %collective-permute-start.1 = (f32[128,128]{1,0:T(8,128)S(1)}, f32[128,128]{1,0:T(8,128)S(1)}, u32[]{:S(2)}, u32[]{:S(2)}) collective-permute-start(f32[128,128]{1,0:T(8,128)S(1)} %get-tuple-element.15.down), channel_id=1, source_target_pairs={{0,31},{1,0},{2,1},{3,2},{4,3},{5,4},{6,5},{7,6},{8,7},{9,8},{10,9... | collective-permute-start | bytes 196616 | tf_op jit(solution)/shard_map/ppermute | solution.py:357
  18.2 1.5 %slab_fields.1 = (f32[4,4,32,128]{3,2,1,0:T(8,128)S(1)}, f32[8,128]{1,0:T(8,128)S(1)}) custom-call(s32[1]{0:T(128)} %bitcast.row_ref, f32[2,16,4,16,128]{4,3,2,1,0:T(8,128)} %vectors.3, f32[4,16,128]{2,1,0:T(8,128)} %potential.3), custom_call_target="tpu_custom_call" | custom-call | flops 1048576 | bytes 524288 | tf_op jit(solution)/shard_map/slab_fields/pallas_call | solution.py:326
  19.7 0.0 collective-permute-done.1.above
  19.7 0.0 collective-permute-done.below
  19.7 0.6 %krylov_gram.1 = (f32[16,128]{1,0:T(8,128)S(1)}, f32[4,2,32,128]{3,2,1,0:T(8,128)S(1)}) custom-call(f32[4,4,32,128]{3,2,1,0:T(8,128)S(1)} %get-tuple-element.12.inside, f32[8,128]{1,0:T(8,128)S(1)} %get-tuple-element.13.diagonals, f32[168,128]{1,0:T(8,128)S(1)} %collective-permute-done.below, f32[128,128]{1,0:T(8,128)S(1)} %collective-permute-done.1.above, ...), custom_call_target="tpu_custom_call" | custom-call | flops 1048576 | bytes 524288 | tf_op jit(solution)/shard_map/krylov_gram/pallas_call | solution.py:326
  20.3 15.5 %all_to_all.10 = f32[32,16,128]{2,1,0:T(8,128)S(1)} all-to-all(f32[32,16,128]{2,1,0:T(8,128)S(1)} %broadcast_in_dim.6), channel_id=1, replica_groups=mesh['x'=4,'zlo'=2,'core'=2,'y'=8,'zhi'=4] {'x','zlo','zhi'}, dimensions={0} | all-to-all | bytes 524288 | tf_op jit(solution)/shard_map/all_to_all | solution.py:370
  35.8 18.0 %all_to_all.11 = f32[16,16,128]{2,1,0:T(8,128)S(1)} all-to-all(f32[16,16,128]{2,1,0:T(8,128)S(1)} %broadcast_in_dim.7), channel_id=1, replica_groups=mesh['x'=4,'zlo'=2,'core'=2,'y'=8,'zhi'=4] {'core','y'}, dimensions={0} | all-to-all | bytes 262144 | tf_op jit(solution)/shard_map/all_to_all | solution.py:370
  53.9 1.1 %combine.1 = (f32[2,16,4,128]{3,2,1,0:T(4,128)}, f32[2,16,16]{2,1,0:T(8,128)}, f32[2,16,16]{2,1,0:T(8,128)}) custom-call(f32[16,128]{1,0:T(8,128)S(1)} %reduce_sum.19.total, f32[4,4,32,128]{3,2,1,0:T(8,128)S(1)} %get-tuple-element.12.inside, f32[4,2,32,128]{3,2,1,0:T(8,128)S(1)} %get-tuple-element.17.fields), custom_call_target="tpu_custom_call" | custom-call | flops 1048576 | bytes 524288 | tf_op jit(solution)/shard_map/combine/pallas_call | solution.py:326
  (4 shorter events, 0.1 us)
Async XLA Ops:
  1.8 17.8 %collective-permute-start = (f32[168,128]{1,0:T(8,128)S(1)}, f32[168,128]{1,0:T(8,128)S(1)}, u32[]{:S(2)}, u32[]{:S(2)}) collective-permute-start(f32[168,128]{1,0:T(8,128)S(1)} %get-tuple-element.14), channel_id=1, source_target_pairs={{0,1},{1,2},{2,3},{3,4},{4,5},{5,6},{6,7},{7,8},{8,9},{9,10},{10,1... | collective-permute-start | bytes 258056 | tf_op jit(solution)/shard_map/ppermute | solution.py:356
  8.5 11.2 %collective-permute-start.1 = (f32[128,128]{1,0:T(8,128)S(1)}, f32[128,128]{1,0:T(8,128)S(1)}, u32[]{:S(2)}, u32[]{:S(2)}) collective-permute-start(f32[128,128]{1,0:T(8,128)S(1)} %get-tuple-element.15.down), channel_id=1, source_target_pairs={{0,31},{1,0},{2,1},{3,2},{4,3},{5,4},{6,5},{7,6},{8,7},{9,8},{10,9... | collective-permute-start | bytes 196616 | tf_op jit(solution)/shard_map/ppermute | solution.py:357

commit v4 on v3

--- a/solution.py
+++ b/solution.py
@@ -16,8 +16,8 @@
 ROWS = 2 * NB
 NZ = 4
 NX = 16
-EDGE = {3: (-2, -1, 0, 1, 2), 2: (-1, 0, 1), 1: (0, 1), 0: (-1, 0, 1, 2)}
-WIDE = {z: (-2, -1, 0, 1, 2, 3) for z in (0, 1, 2, 3)}
+EDGE = {3: (-2, -1, 0, 1, 2), 2: (-1, 0, 1), 1: (0,), 0: (-1, 0, 1)}
+WIDE = {z: ((-3,) if z > 1 else ()) + (-2, -1, 0, 1, 2, 3) for z in (0, 1, 2, 3)}
 PHASES = (("x", "zlo", "zhi"), ("core", "y"))
 POLE = ("x", "zlo", "core")
 SLAB = ("y", "zhi")
@@ -62,6 +62,10 @@
             beside = beside + v(z + 1, k)
         return self.diagonal(z, k) * v(z, k) - 0.5 * beside
 
+    def into_next(self, v, z, inner, k):
+        around = turned(v(z, k)) + (v(z, k - 1) + v(z, k + 1))
+        return 0.5 * (around - self.diagonal(z, k) * v(z, k)) + 0.25 * v(inner, k)
+
 
 def slab_edges(row_ref, vectors, potential, up, down, buffer, levels, sems):
     row = row_ref[0]
@@ -75,24 +79,24 @@
     def field(z, k):
         return buffer[slots[z, k]].reshape(ROWS, 128)
 
-    def into_next(z, inner, k):
-        around = turned(field(z, k)) + (field(z, k - 1) + field(z, k + 1))
-        return 0.5 * (around - slab.diagonal(z, k) * field(z, k)) + 0.25 * field(inner, k)
-
     first = {}
     for z, k in [(2, 0), (3, -1), (3, 0), (3, 1)]:
         first[z, k] = slab.apply(field, z, k)
     second = slab.apply(lambda z, k: first[z, k], 3, 0) + 0.25 * field(3, 0)
-    out = [field(3, 0), field(3, 1), into_next(3, 2, 0), into_next(3, 2, 1), second]
+    out = [field(3, 0), field(3, 1)]
+    out += [slab.into_next(field, 3, 2, k) for k in (0, 1)] + [second]
     for i, block in enumerate(out):
         up[pl.ds(i * ROWS, ROWS), :] = block
-    up[pl.ds(len(out) * ROWS, 8), :] = jnp.broadcast_to(slab.diagonal(3, 0), (8, 128))
-    out = [field(0, 0), field(0, 1), into_next(0, 1, 0), into_next(0, 1, 1)]
+    for k in (0, 1):
+        up[pl.ds(len(out) * ROWS + 8 * k, 8), :] = jnp.broadcast_to(slab.diagonal(3, k), (8, 128))
+    out = [field(0, 0), slab.into_next(field, 0, 1, 0)]
     for i, block in enumerate(out):
         down[pl.ds(i * ROWS, ROWS), :] = block
 
 
-def slab_fields(row_ref, vectors, potential, inside, diagonals, buffer, levels, sems):
+def slab_fields(
+    row_ref, vectors, potential, inside, beside, diagonals, buffer, levels, sems
+):
     row = row_ref[0]
     level_copy = pltpu.make_async_copy(potential, levels, sems.at[sum(map(len, WIDE.values()))])
     level_copy.start()
@@ -106,8 +110,14 @@
 
     first = {}
     for z in range(NZ):
-        for k in (-1, 0, 1, 2):
+        for k in ((-2,) if z > 1 else ()) + (-1, 0, 1, 2):
             first[z, k] = slab.apply(field, z, k)
+    for k in (0, 1):
+        beside[k] = slab.into_next(field, 0, 1, k)
+        beside[2 + k] = 0.25 * field(0, k)
+    for z in (2, 3):
+        second = slab.apply(lambda z, k: first[z, k], z, -1)
+        beside[2 + z] = second + 0.25 * field(z, -1) if z == NZ - 1 else second
     for z in range(NZ):
         inside[z, 0] = field(z, 0)
         inside[z, 1] = first[z, 0]
@@ -119,25 +129,34 @@
             diagonals[pl.ds(2 * z + k, 1), :] = slab.diagonal(z, k)
 
 
-def krylov_gram(inside, diagonals, below, above, down, packed, fields, stack):
+def krylov_gram(
+    inside, beside, diagonals, below, above, packed, fields, stack, seams
+):
     def part(halo, i):
         return halo[pl.ds(i * ROWS, ROWS), :]
 
     def level(z, k):
         return diagonals[pl.ds(2 * z + k, 1), :]
 
-    v1, v2 = {}, {}
+    v1, v2, add = {}, {}, {}
     for z in range(NZ):
         v1[z] = inside[z, 1]
         for k in (0, 1):
             v2[z, k] = inside[z, 2 + k]
-    for z, near, halo in [(0, 1, below), (3, 2, above)]:
-        v1[z] = v1[z] - 0.5 * part(halo, 0)
-        for k in (0, 1):
-            v2[z, k] = v2[z, k] + (part(halo, 2 + k) - 0.5 * (level(z, k) * part(halo, k)))
-            v2[near, k] = v2[near, k] + 0.25 * part(halo, k)
-    lowest = below[pl.ds(5 * ROWS, 1), :]
-    v2[-1, 0] = part(below, 4) + (part(down, 2) - 0.5 * (lowest * part(down, 0)))
+    v1[0] = v1[0] - 0.5 * part(below, 0)
+    v1[3] = v1[3] - 0.5 * part(above, 0)
+    for k in (0, 1):
+        add[0, k] = part(below, 2 + k) - 0.5 * (level(0, k) * part(below, k))
+        add[1, k] = 0.25 * part(below, k)
+    add[3, 0] = part(above, 1) - 0.5 * (level(3, 0) * part(above, 0))
+    add[2, 0] = 0.25 * part(above, 0)
+    for at, value in add.items():
+        v2[at] = v2[at] + value
+    given = []
+    for k in (0, 1):
+        lowest = below[pl.ds(5 * ROWS + 8 * k, 1), :]
+        given.append(beside[k] - 2.0 * (lowest * beside[2 + k]))
+    v2[-1, 0] = part(below, 4) + given[0]
     for z in range(NZ):
         here = v2[z, 0]
         ahead = v2[z - 1, 0] + v2[z, 1] + pltpu.roll(here, 127, 1)
@@ -146,13 +165,24 @@
         fields[z, 1] = here
         for i, block in enumerate((inside[z, 0], v1[z], here, half)):
             stack[pl.ds(i * ROWS, ROWS), pl.ds(z * 128, 128)] = block
-    gram = lax.dot_general(
-        stack[...],
-        stack[...],
-        (((1,), (1,)), ((), ())),
-        precision=lax.Precision.HIGHEST,
-        preferred_element_type=jnp.float32,
-    )
+    pairs = [(add[2, 0], beside[4]), (add[3, 0], beside[5]), (given[0], given[1])]
+    pairs.append((beside[2], beside[3]))
+    seams[pl.ds(0, 2 * ROWS), :] = jnp.zeros((2 * ROWS, NZ * 128), jnp.float32)
+    for i, (one, other) in enumerate(pairs):
+        seams[pl.ds(2 * ROWS, ROWS), pl.ds(i * 128, 128)] = one
+        seams[pl.ds(3 * ROWS, ROWS), pl.ds(i * 128, 128)] = -0.5 * other
+
+    def outer(a, b):
+        return lax.dot_general(
+            a,
+            b,
+            (((1,), (1,)), ((), ())),
+            precision=lax.Precision.HIGHEST,
+            preferred_element_type=jnp.float32,
+        )
+
+    gram = outer(stack[...], stack[...])
+    seam = outer(seams[pl.ds(2 * ROWS, 2 * ROWS), :], seams[...])
     lane = lax.broadcasted_iota(jnp.int32, (NB, 128), 1)
     sub = lax.broadcasted_iota(jnp.int32, (NB, 128), 0)
     result = jnp.zeros((NB, 128), jnp.float32)
@@ -162,6 +192,9 @@
         for i, j in parts:
             top = gram[ROWS * i : ROWS * i + NB, :]
             low = gram[ROWS * i + NB : ROWS * i + ROWS, :]
+            if n == 5:
+                top = top + seam[ROWS * (i - 2) : ROWS * (i - 2) + NB, :]
+                low = low + seam[ROWS * (i - 2) + NB : ROWS * (i - 2) + ROWS, :]
             first = (NB * n - ROWS * j) % 128
             second = (NB * n - ROWS * j - NB) % 128
             rr = rr + (pltpu.roll(top, first, 1) if first else top)
@@ -350,19 +383,22 @@
 
     source = (("s", row), ("h", vectors), ("h", potential))
     up, down = call(
-        slab_edges, [(5 * ROWS + 8, 128), (4 * ROWS, 128)], scratch(EDGE), *source
+        slab_edges, [(5 * ROWS + 16, 128), (2 * ROWS, 128)], scratch(EDGE), *source
     )
     slabs = lax.axis_size(SLAB)
     below = lax.ppermute(up, SLAB, [(i, (i + 1) % slabs) for i in range(slabs)])
     above = lax.ppermute(down, SLAB, [(i, (i - 1) % slabs) for i in range(slabs)])
-    inside, diagonals = call(
-        slab_fields, [(NZ, 4, ROWS, 128), (2 * NZ, 128)], scratch(WIDE), *source
+    inside, beside, diagonals = call(
+        slab_fields,
+        [(NZ, 4, ROWS, 128), (6, ROWS, 128), (2 * NZ, 128)],
+        scratch(WIDE),
+        *source,
     )
     packed, fields = call(
         krylov_gram,
         [(NB, 128), (NZ, 2, ROWS, 128)],
-        [pltpu.VMEM((4 * ROWS, NZ * 128), jnp.float32)],
-        *(("v", a) for a in (inside, diagonals, below, above, down)),
+        [pltpu.VMEM((4 * ROWS, NZ * 128), jnp.float32)] * 2,
+        *(("v", a) for a in (inside, beside, diagonals, below, above)),
     )
     for axes in PHASES:
         count = lax.axis_size(axes)

time: 55.4 us -> 55 us (level)
  blocking collectives: 33.5 us -> 32.8 us
    all_to_all x2, blocking collectives: 33.5 us -> 32.8 us  [on_device(): packed = jnp.sum(lax.all_to_all(shared, axes, 0, 0), axis=0)]
where the time goes in v4:
time: 55 us; the launch traced here: 54.6 us
  blocking collectives  32.8 us (60%)
  starting transfers between devices  16.3 us (30%)
  Pallas kernels  4.69 us (9%)
  between operations  0.71 us (1%)
    all_to_all x2, blocking collectives, on_device(): packed = jnp.sum(lax.all_to_all(shared, axes, 0, 0), axis=0)  32.8 us
    ppermute x1, starting transfers between devices, on_device(): lax.ppermute(down, SLAB, [(i, (i - 1) % slabs) for i in range(slabs)])  9.67 us
    ppermute x1, starting transfers between devices, on_device(): below = lax.ppermute(up, SLAB, [(i, (i + 1) % slabs) for i in range(slabs)])  6.64 us
    pallas_call x4, Pallas kernels, call(): pl.pallas_call(kernel, in_specs=[pl.BlockSpec(memory_space=space[kind]) f...  4.69 us
  transfers between devices with their start and end apart: 2, of which 0 were waited for; matrix products, arithmetic and copies ran while one was open for 0% of the time, Pallas kernels for 3%

profile of v4, /device:TPU:1, one launch (start us, length us, event | category | flops | bytes accessed | tf_op | source)
XLA Modules:
  0.0 54.6 jit_solution(11724401982744686657)
XLA Ops:
  0.6 1.2 %slab_edges.1 = (f32[176,128]{1,0:T(8,128)S(1)}, f32[64,128]{1,0:T(8,128)S(1)}) custom-call(s32[1]{0:T(128)} %bitcast.row_ref, f32[2,16,4,16,128]{4,3,2,1,0:T(8,128)} %vectors.3, f32[4,16,128]{2,1,0:T(8,128)} %potential.3), custom_call_target="tpu_custom_call" | custom-call | flops 1048576 | bytes 524288 | tf_op jit(solution)/shard_map/slab_edges/pallas_call | solution.py:359
  1.8 6.6 %collective-permute-start = (f32[176,128]{1,0:T(8,128)S(1)}, f32[176,128]{1,0:T(8,128)S(1)}, u32[]{:S(2)}, u32[]{:S(2)}) collective-permute-start(f32[176,128]{1,0:T(8,128)S(1)} %get-tuple-element.16), channel_id=1, source_target_pairs={{0,1},{1,2},{2,3},{3,4},{4,5},{5,6},{6,7},{7,8},{8,9},{9,10},{10,1... | collective-permute-start | bytes 270344 | tf_op jit(solution)/shard_map/ppermute | solution.py:389
  8.5 9.7 %collective-permute-start.1 = (f32[64,128]{1,0:T(8,128)S(1)}, f32[64,128]{1,0:T(8,128)S(1)}, u32[]{:S(2)}, u32[]{:S(2)}) collective-permute-start(f32[64,128]{1,0:T(8,128)S(1)} %get-tuple-element.17), channel_id=1, source_target_pairs={{0,31},{1,0},{2,1},{3,2},{4,3},{5,4},{6,5},{7,6},{8,7},{9,8},{10,9... | collective-permute-start | bytes 98312 | tf_op jit(solution)/shard_map/ppermute | solution.py:390
  18.1 1.6 %slab_fields.1 = (f32[4,4,32,128]{3,2,1,0:T(8,128)S(1)}, f32[6,32,128]{2,1,0:T(8,128)S(1)}, f32[8,128]{1,0:T(8,128)S(1)}) custom-call(s32[1]{0:T(128)} %bitcast.row_ref, f32[2,16,4,16,128]{4,3,2,1,0:T(8,128)} %vectors.3, f32[4,16,128]{2,1,0:T(8,128)} %potential.3), custom_call_target="tpu_custom_call" | custom-call | flops 1048576 | bytes 524288 | tf_op jit(solution)/shard_map/slab_fields/pallas_call | solution.py:359
  19.8 0.0 collective-permute-done.1.above
  19.8 0.0 collective-permute-done.below
  19.8 0.8 %krylov_gram.1 = (f32[16,128]{1,0:T(8,128)S(1)}, f32[4,2,32,128]{3,2,1,0:T(8,128)S(1)}) custom-call(f32[4,4,32,128]{3,2,1,0:T(8,128)S(1)} %get-tuple-element.13.inside, f32[6,32,128]{2,1,0:T(8,128)S(1)} %get-tuple-element.14.beside, f32[8,128]{1,0:T(8,128)S(1)} %get-tuple-element.15.diagonals, f32[176,128]{1,0:T(8,128)S(1)} %collective-permute-done.below, ...), custom_call_target="tpu_custom_call" | custom-call | flops 1048576 | bytes 524288 | tf_op jit(solution)/shard_map/krylov_gram/pallas_call | solution.py:359
  20.6 14.6 %all_to_all.10 = f32[32,16,128]{2,1,0:T(8,128)S(1)} all-to-all(f32[32,16,128]{2,1,0:T(8,128)S(1)} %broadcast_in_dim.6), channel_id=1, replica_groups=mesh['x'=4,'zlo'=2,'core'=2,'y'=8,'zhi'=4] {'x','zlo','zhi'}, dimensions={0} | all-to-all | bytes 524288 | tf_op jit(solution)/shard_map/all_to_all | solution.py:406
  35.3 18.1 %all_to_all.11 = f32[16,16,128]{2,1,0:T(8,128)S(1)} all-to-all(f32[16,16,128]{2,1,0:T(8,128)S(1)} %broadcast_in_dim.7), channel_id=1, replica_groups=mesh['x'=4,'zlo'=2,'core'=2,'y'=8,'zhi'=4] {'core','y'}, dimensions={0} | all-to-all | bytes 262144 | tf_op jit(solution)/shard_map/all_to_all | solution.py:406
  53.5 1.1 %combine.1 = (f32[2,16,4,128]{3,2,1,0:T(4,128)}, f32[2,16,16]{2,1,0:T(8,128)}, f32[2,16,16]{2,1,0:T(8,128)}) custom-call(f32[16,128]{1,0:T(8,128)S(1)} %reduce_sum.19.total, f32[4,4,32,128]{3,2,1,0:T(8,128)S(1)} %get-tuple-element.13.inside, f32[4,2,32,128]{3,2,1,0:T(8,128)S(1)} %get-tuple-element.19.fields), custom_call_target="tpu_custom_call" | custom-call | flops 1048576 | bytes 524288 | tf_op jit(solution)/shard_map/combine/pallas_call | solution.py:359
  (4 shorter events, 0.1 us)
Async XLA Ops:
  1.8 17.9 %collective-permute-start = (f32[176,128]{1,0:T(8,128)S(1)}, f32[176,128]{1,0:T(8,128)S(1)}, u32[]{:S(2)}, u32[]{:S(2)}) collective-permute-start(f32[176,128]{1,0:T(8,128)S(1)} %get-tuple-element.16), channel_id=1, source_target_pairs={{0,1},{1,2},{2,3},{3,4},{4,5},{5,6},{6,7},{7,8},{8,9},{9,10},{10,1... | collective-permute-start | bytes 270344 | tf_op jit(solution)/shard_map/ppermute | solution.py:389
  8.5 11.3 %collective-permute-start.1 = (f32[64,128]{1,0:T(8,128)S(1)}, f32[64,128]{1,0:T(8,128)S(1)}, u32[]{:S(2)}, u32[]{:S(2)}) collective-permute-start(f32[64,128]{1,0:T(8,128)S(1)} %get-tuple-element.17), channel_id=1, source_target_pairs={{0,31},{1,0},{2,1},{3,2},{4,3},{5,4},{6,5},{7,6},{8,7},{9,8},{10,9... | collective-permute-start | bytes 98312 | tf_op jit(solution)/shard_map/ppermute | solution.py:390

commit v5 on v4

--- a/solution.py
+++ b/solution.py
@@ -167,10 +167,9 @@
             stack[pl.ds(i * ROWS, ROWS), pl.ds(z * 128, 128)] = block
     pairs = [(add[2, 0], beside[4]), (add[3, 0], beside[5]), (given[0], given[1])]
     pairs.append((beside[2], beside[3]))
-    seams[pl.ds(0, 2 * ROWS), :] = jnp.zeros((2 * ROWS, NZ * 128), jnp.float32)
     for i, (one, other) in enumerate(pairs):
-        seams[pl.ds(2 * ROWS, ROWS), pl.ds(i * 128, 128)] = one
-        seams[pl.ds(3 * ROWS, ROWS), pl.ds(i * 128, 128)] = -0.5 * other
+        seams[pl.ds(0, ROWS), pl.ds(i * 128, 128)] = one
+        seams[pl.ds(ROWS, ROWS), pl.ds(i * 128, 128)] = -0.5 * other
 
     def outer(a, b):
         return lax.dot_general(
@@ -182,7 +181,8 @@
         )
 
     gram = outer(stack[...], stack[...])
-    seam = outer(seams[pl.ds(2 * ROWS, 2 * ROWS), :], seams[...])
+    seam = outer(seams[...], seams[...])
+    seam = jnp.concatenate([jnp.zeros((2 * ROWS, 2 * ROWS), jnp.float32), seam], axis=1)
     lane = lax.broadcasted_iota(jnp.int32, (NB, 128), 1)
     sub = lax.broadcasted_iota(jnp.int32, (NB, 128), 0)
     result = jnp.zeros((NB, 128), jnp.float32)
@@ -397,7 +397,7 @@
     packed, fields = call(
         krylov_gram,
         [(NB, 128), (NZ, 2, ROWS, 128)],
-        [pltpu.VMEM((4 * ROWS, NZ * 128), jnp.float32)] * 2,
+        [pltpu.VMEM((rows * ROWS, NZ * 128), jnp.float32) for rows in (4, 2)],
         *(("v", a) for a in (inside, beside, diagonals, below, above)),
     )
     for axes in PHASES:

time: 55 us -> 54.9 us (level)
  no operation moved by 1% of the time
where the time goes in v5:
time: 54.9 us; the launch traced here: 54.6 us
  blocking collectives  32.8 us (60%)
  starting transfers between devices  16.3 us (30%)
  Pallas kernels  4.64 us (8%)
  between operations  0.71 us (1%)
    all_to_all x2, blocking collectives, on_device(): packed = jnp.sum(lax.all_to_all(shared, axes, 0, 0), axis=0)  32.8 us
    ppermute x1, starting transfers between devices, on_device(): lax.ppermute(down, SLAB, [(i, (i - 1) % slabs) for i in range(slabs)])  9.67 us
    ppermute x1, starting transfers between devices, on_device(): below = lax.ppermute(up, SLAB, [(i, (i + 1) % slabs) for i in range(slabs)])  6.64 us
    pallas_call x4, Pallas kernels, call(): pl.pallas_call(kernel, in_specs=[pl.BlockSpec(memory_space=space[kind]) f...  4.64 us
  transfers between devices with their start and end apart: 2, of which 0 were waited for; matrix products, arithmetic and copies ran while one was open for 0% of the time, Pallas kernels for 3%

profile of v5, /device:TPU:1, one launch (start us, length us, event | category | flops | bytes accessed | tf_op | source)
XLA Modules:
  0.0 54.6 jit_solution(11751511044645658236)
XLA Ops:
  0.6 1.2 %slab_edges.1 = (f32[176,128]{1,0:T(8,128)S(1)}, f32[64,128]{1,0:T(8,128)S(1)}) custom-call(s32[1]{0:T(128)} %bitcast.row_ref, f32[2,16,4,16,128]{4,3,2,1,0:T(8,128)} %vectors.3, f32[4,16,128]{2,1,0:T(8,128)} %potential.3), custom_call_target="tpu_custom_call" | custom-call | flops 1048576 | bytes 524288 | tf_op jit(solution)/shard_map/slab_edges/pallas_call | solution.py:359
  1.8 6.6 %collective-permute-start = (f32[176,128]{1,0:T(8,128)S(1)}, f32[176,128]{1,0:T(8,128)S(1)}, u32[]{:S(2)}, u32[]{:S(2)}) collective-permute-start(f32[176,128]{1,0:T(8,128)S(1)} %get-tuple-element.16), channel_id=1, source_target_pairs={{0,1},{1,2},{2,3},{3,4},{4,5},{5,6},{6,7},{7,8},{8,9},{9,10},{10,1... | collective-permute-start | bytes 270344 | tf_op jit(solution)/shard_map/ppermute | solution.py:389
  8.5 9.7 %collective-permute-start.1 = (f32[64,128]{1,0:T(8,128)S(1)}, f32[64,128]{1,0:T(8,128)S(1)}, u32[]{:S(2)}, u32[]{:S(2)}) collective-permute-start(f32[64,128]{1,0:T(8,128)S(1)} %get-tuple-element.17), channel_id=1, source_target_pairs={{0,31},{1,0},{2,1},{3,2},{4,3},{5,4},{6,5},{7,6},{8,7},{9,8},{10,9... | collective-permute-start | bytes 98312 | tf_op jit(solution)/shard_map/ppermute | solution.py:390
  18.1 1.6 %slab_fields.1 = (f32[4,4,32,128]{3,2,1,0:T(8,128)S(1)}, f32[6,32,128]{2,1,0:T(8,128)S(1)}, f32[8,128]{1,0:T(8,128)S(1)}) custom-call(s32[1]{0:T(128)} %bitcast.row_ref, f32[2,16,4,16,128]{4,3,2,1,0:T(8,128)} %vectors.3, f32[4,16,128]{2,1,0:T(8,128)} %potential.3), custom_call_target="tpu_custom_call" | custom-call | flops 1048576 | bytes 524288 | tf_op jit(solution)/shard_map/slab_fields/pallas_call | solution.py:359
  19.8 0.0 collective-permute-done.1.above
  19.8 0.0 collective-permute-done.below
  19.8 0.8 %krylov_gram.1 = (f32[16,128]{1,0:T(8,128)S(1)}, f32[4,2,32,128]{3,2,1,0:T(8,128)S(1)}) custom-call(f32[4,4,32,128]{3,2,1,0:T(8,128)S(1)} %get-tuple-element.13.inside, f32[6,32,128]{2,1,0:T(8,128)S(1)} %get-tuple-element.14.beside, f32[8,128]{1,0:T(8,128)S(1)} %get-tuple-element.15.diagonals, f32[176,128]{1,0:T(8,128)S(1)} %collective-permute-done.below, ...), custom_call_target="tpu_custom_call" | custom-call | flops 1048576 | bytes 524288 | tf_op jit(solution)/shard_map/krylov_gram/pallas_call | solution.py:359
  20.6 14.6 %all_to_all.10 = f32[32,16,128]{2,1,0:T(8,128)S(1)} all-to-all(f32[32,16,128]{2,1,0:T(8,128)S(1)} %broadcast_in_dim.6), channel_id=1, replica_groups=mesh['x'=4,'zlo'=2,'core'=2,'y'=8,'zhi'=4] {'x','zlo','zhi'}, dimensions={0} | all-to-all | bytes 524288 | tf_op jit(solution)/shard_map/all_to_all | solution.py:406
  35.3 18.2 %all_to_all.11 = f32[16,16,128]{2,1,0:T(8,128)S(1)} all-to-all(f32[16,16,128]{2,1,0:T(8,128)S(1)} %broadcast_in_dim.7), channel_id=1, replica_groups=mesh['x'=4,'zlo'=2,'core'=2,'y'=8,'zhi'=4] {'core','y'}, dimensions={0} | all-to-all | bytes 262144 | tf_op jit(solution)/shard_map/all_to_all | solution.py:406
  53.4 1.1 %combine.1 = (f32[2,16,4,128]{3,2,1,0:T(4,128)}, f32[2,16,16]{2,1,0:T(8,128)}, f32[2,16,16]{2,1,0:T(8,128)}) custom-call(f32[16,128]{1,0:T(8,128)S(1)} %reduce_sum.19.total, f32[4,4,32,128]{3,2,1,0:T(8,128)S(1)} %get-tuple-element.13.inside, f32[4,2,32,128]{3,2,1,0:T(8,128)S(1)} %get-tuple-element.19.fields), custom_call_target="tpu_custom_call" | custom-call | flops 1048576 | bytes 524288 | tf_op jit(solution)/shard_map/combine/pallas_call | solution.py:359
  (4 shorter events, 0.1 us)
Async XLA Ops:
  1.8 17.9 %collective-permute-start = (f32[176,128]{1,0:T(8,128)S(1)}, f32[176,128]{1,0:T(8,128)S(1)}, u32[]{:S(2)}, u32[]{:S(2)}) collective-permute-start(f32[176,128]{1,0:T(8,128)S(1)} %get-tuple-element.16), channel_id=1, source_target_pairs={{0,1},{1,2},{2,3},{3,4},{4,5},{5,6},{6,7},{7,8},{8,9},{9,10},{10,1... | collective-permute-start | bytes 270344 | tf_op jit(solution)/shard_map/ppermute | solution.py:389
  8.5 11.3 %collective-permute-start.1 = (f32[64,128]{1,0:T(8,128)S(1)}, f32[64,128]{1,0:T(8,128)S(1)}, u32[]{:S(2)}, u32[]{:S(2)}) collective-permute-start(f32[64,128]{1,0:T(8,128)S(1)} %get-tuple-element.17), channel_id=1, source_target_pairs={{0,31},{1,0},{2,1},{3,2},{4,3},{5,4},{6,5},{7,6},{8,7},{9,8},{10,9... | collective-permute-start | bytes 98312 | tf_op jit(solution)/shard_map/ppermute | solution.py:390

commit v6 on v5

--- a/solution.py
+++ b/solution.py
@@ -230,7 +230,7 @@
 
 
 def combine(poles, cells, total, inside, fields, filtered, correlation, energy):
-    moments = total[...]
+    moments = jnp.sum(total[...], axis=0)
     lane = lax.broadcasted_iota(jnp.int32, (NB, 128), 1)
     m = [
         tuple(
@@ -403,7 +403,8 @@
     for axes in PHASES:
         count = lax.axis_size(axes)
         shared = jnp.broadcast_to(packed[None], (count, NB, 128))
-        packed = jnp.sum(lax.all_to_all(shared, axes, 0, 0), axis=0)
+        received = lax.all_to_all(shared, axes, 0, 0)
+        packed = received if axes == PHASES[-1] else jnp.sum(received, axis=0)
     cells = NZ * slabs * NX * 128
     filtered, correlation, energy = call(
         functools.partial(combine, lax.axis_size(POLE), cells),

time: 54.9 us -> 54.9 us (level)
  no operation moved by 1% of the time
where the time goes in v6:
time: 54.9 us; the launch traced here: 54.6 us
  blocking collectives  32.8 us (60%)
  starting transfers between devices  16.3 us (30%)
  Pallas kernels  4.65 us (8%)
  between operations  0.71 us (1%)
    all_to_all x2, blocking collectives, on_device(): received = lax.all_to_all(shared, axes, 0, 0)  32.8 us
    ppermute x1, starting transfers between devices, on_device(): lax.ppermute(down, SLAB, [(i, (i - 1) % slabs) for i in range(slabs)])  9.67 us
    ppermute x1, starting transfers between devices, on_device(): below = lax.ppermute(up, SLAB, [(i, (i + 1) % slabs) for i in range(slabs)])  6.64 us
    pallas_call x4, Pallas kernels, call(): pl.pallas_call(kernel, in_specs=[pl.BlockSpec(memory_space=space[kind]) f...  4.65 us
  transfers between devices with their start and end apart: 2, of which 0 were waited for; matrix products, arithmetic and copies ran while one was open for 0% of the time, Pallas kernels for 3%

profile of v6, /device:TPU:1, one launch (start us, length us, event | category | flops | bytes accessed | tf_op | source)
XLA Modules:
  0.0 54.6 jit_solution(10061104092402014883)
XLA Ops:
  0.6 1.2 %slab_edges.1 = (f32[176,128]{1,0:T(8,128)S(1)}, f32[64,128]{1,0:T(8,128)S(1)}) custom-call(s32[1]{0:T(128)} %bitcast.row_ref, f32[2,16,4,16,128]{4,3,2,1,0:T(8,128)} %vectors.3, f32[4,16,128]{2,1,0:T(8,128)} %potential.3), custom_call_target="tpu_custom_call" | custom-call | flops 1048576 | bytes 524288 | tf_op jit(solution)/shard_map/slab_edges/pallas_call | solution.py:359
  1.8 6.6 %collective-permute-start = (f32[176,128]{1,0:T(8,128)S(1)}, f32[176,128]{1,0:T(8,128)S(1)}, u32[]{:S(2)}, u32[]{:S(2)}) collective-permute-start(f32[176,128]{1,0:T(8,128)S(1)} %get-tuple-element.16), channel_id=1, source_target_pairs={{0,1},{1,2},{2,3},{3,4},{4,5},{5,6},{6,7},{7,8},{8,9},{9,10},{10,1... | collective-permute-start | bytes 270344 | tf_op jit(solution)/shard_map/ppermute | solution.py:389
  8.5 9.7 %collective-permute-start.1 = (f32[64,128]{1,0:T(8,128)S(1)}, f32[64,128]{1,0:T(8,128)S(1)}, u32[]{:S(2)}, u32[]{:S(2)}) collective-permute-start(f32[64,128]{1,0:T(8,128)S(1)} %get-tuple-element.17), channel_id=1, source_target_pairs={{0,31},{1,0},{2,1},{3,2},{4,3},{5,4},{6,5},{7,6},{8,7},{9,8},{10,9... | collective-permute-start | bytes 98312 | tf_op jit(solution)/shard_map/ppermute | solution.py:390
  18.1 1.6 %slab_fields.1 = (f32[4,4,32,128]{3,2,1,0:T(8,128)S(1)}, f32[6,32,128]{2,1,0:T(8,128)S(1)}, f32[8,128]{1,0:T(8,128)S(1)}) custom-call(s32[1]{0:T(128)} %bitcast.row_ref, f32[2,16,4,16,128]{4,3,2,1,0:T(8,128)} %vectors.3, f32[4,16,128]{2,1,0:T(8,128)} %potential.3), custom_call_target="tpu_custom_call" | custom-call | flops 1048576 | bytes 524288 | tf_op jit(solution)/shard_map/slab_fields/pallas_call | solution.py:359
  19.8 0.0 collective-permute-done.1.above
  19.8 0.0 collective-permute-done.below
  19.8 0.8 %krylov_gram.1 = (f32[16,128]{1,0:T(8,128)S(1)}, f32[4,2,32,128]{3,2,1,0:T(8,128)S(1)}) custom-call(f32[4,4,32,128]{3,2,1,0:T(8,128)S(1)} %get-tuple-element.13.inside, f32[6,32,128]{2,1,0:T(8,128)S(1)} %get-tuple-element.14.beside, f32[8,128]{1,0:T(8,128)S(1)} %get-tuple-element.15.diagonals, f32[176,128]{1,0:T(8,128)S(1)} %collective-permute-done.below, ...), custom_call_target="tpu_custom_call" | custom-call | flops 1048576 | bytes 524288 | tf_op jit(solution)/shard_map/krylov_gram/pallas_call | solution.py:359
  20.6 14.6 %all_to_all.10 = f32[32,16,128]{2,1,0:T(8,128)S(1)} all-to-all(f32[32,16,128]{2,1,0:T(8,128)S(1)} %broadcast_in_dim.6), channel_id=1, replica_groups=mesh['x'=4,'zlo'=2,'core'=2,'y'=8,'zhi'=4] {'x','zlo','zhi'}, dimensions={0} | all-to-all | bytes 524288 | tf_op jit(solution)/shard_map/all_to_all | solution.py:406
  35.3 18.2 %all_to_all.11.total = f32[16,16,128]{2,1,0:T(8,128)S(1)} all-to-all(f32[16,16,128]{2,1,0:T(8,128)S(1)} %broadcast_in_dim.7), channel_id=1, replica_groups=mesh['x'=4,'zlo'=2,'core'=2,'y'=8,'zhi'=4] {'core','y'}, dimensions={0} | all-to-all | bytes 262144 | tf_op jit(solution)/shard_map/all_to_all | solution.py:406
  53.4 1.1 %combine.1 = (f32[2,16,4,128]{3,2,1,0:T(4,128)}, f32[2,16,16]{2,1,0:T(8,128)}, f32[2,16,16]{2,1,0:T(8,128)}) custom-call(f32[16,16,128]{2,1,0:T(8,128)S(1)} %all_to_all.11.total, f32[4,4,32,128]{3,2,1,0:T(8,128)S(1)} %get-tuple-element.13.inside, f32[4,2,32,128]{3,2,1,0:T(8,128)S(1)} %get-tuple-element.19.fields), custom_call_target="tpu_custom_call" | custom-call | flops 1048576 | bytes 524288 | tf_op jit(solution)/shard_map/combine/pallas_call | solution.py:359
  (3 shorter events, 0.1 us)
Async XLA Ops:
  1.8 17.9 %collective-permute-start = (f32[176,128]{1,0:T(8,128)S(1)}, f32[176,128]{1,0:T(8,128)S(1)}, u32[]{:S(2)}, u32[]{:S(2)}) collective-permute-start(f32[176,128]{1,0:T(8,128)S(1)} %get-tuple-element.16), channel_id=1, source_target_pairs={{0,1},{1,2},{2,3},{3,4},{4,5},{5,6},{6,7},{7,8},{8,9},{9,10},{10,1... | collective-permute-start | bytes 270344 | tf_op jit(solution)/shard_map/ppermute | solution.py:389
  8.5 11.3 %collective-permute-start.1 = (f32[64,128]{1,0:T(8,128)S(1)}, f32[64,128]{1,0:T(8,128)S(1)}, u32[]{:S(2)}, u32[]{:S(2)}) collective-permute-start(f32[64,128]{1,0:T(8,128)S(1)} %get-tuple-element.17), channel_id=1, source_target_pairs={{0,31},{1,0},{2,1},{3,2},{4,3},{5,4},{6,5},{7,6},{8,7},{9,8},{10,9... | collective-permute-start | bytes 98312 | tf_op jit(solution)/shard_map/ppermute | solution.py:390
